TPU v7x, 256 devices: a whole 4x4x8 slice. The times are simulated.
256 devices in a mesh: band: 2 (over core), grow: 8 (over z), gcol: 16 (over y, x).
Axes of the slice: x: 4, y: 4, z: 8, core: 2. Of those that a mesh axis runs over, the one named last changes fastest.
Arguments:
- valence_orbitals: bfloat16 [16, 98304], replicated, may hold values from -6 to 6
- conduction_orbitals: bfloat16 [1024, 98304], P(('band', 'grow', 'gcol')), may hold values from -6 to 6
- valence_energy: float32 [16], replicated, may hold values from -3 to -0.5
- conduction_energy: float32 [1024], replicated, may hold values from 0.5 to 3
- coulomb_root: float32 [12288], replicated, may hold values from 0.2 to 2
- pair_bands: int32 [2, 5120], P(None, ('band', 'grow', 'gcol')), may hold values from 0 to 1023, as said below
- slot_counts: int32 [256], P(('band', 'grow', 'gcol')), may hold values from 1 to 19, as said below
Outputs:
- chi_zero: float32 [2, 12288, 12288], P('band', 'grow', 'gcol')
Inputs may be any that keep to these rules, and one draw needn't show every extreme that they name: `pair_bands`: the slots of device d name conduction orbitals d * 4 to (d + 1) * 4 - 1 only, each of them at least once; no (valence, conduction) pair appears in two slots anywhere. `slot_counts`: the two devices of one chip (same grow and gcol index, band 0 and band 1) hold at most 20 live slots together; some chip holds exactly 20, and some device holds exactly 19.
All inputs are finite; a program needn't handle non-finite values.
Results may differ from a plain program's by a relative error of at most 0.012.
Values may be sent and summed in bfloat16 or wider, within the bound.
No kernel may reach another device: no remote copies, remote signals or barrier semaphores. Data moves between devices by JAX's collectives and lax.ppermute only.
A program may use at most 128 MiB of HBM per device.

v0:
```python
import math

import jax
import jax.numpy as jnp
import numpy as np
from jax import lax
from jax.experimental import pallas as pl
from jax.experimental.pallas import tpu as pltpu
from jax.sharding import Mesh
from jax.sharding import PartitionSpec as P


N1, N2, N3 = 16, 24, 32
M1, M2, M3 = 32, 48, 64
NP = N2 * N3
KP = M2 * M3
MG = M1 * KP
ROW = 2 * NP
TOTAL = 5120
SLOTS = 20
HALF = 10
GROW, GCOL = 8, 16
LANES = 128
CHUNKS = KP // LANES
LINES = MG // LANES + 4
PANEL = GROW * GCOL * HALF
BLOCK = 64
ROWBLOCK = 120
COLROWS = GCOL * BLOCK + 4
WIDTH = NP // LANES
STEP = 1536
F32, BF16 = jnp.float32, jnp.bfloat16
VMEM = pltpu.VMEM
SMEM = pltpu.SMEM


def wave_table(keep, length):
    wave = (np.arange(keep)[:, None] - keep // 2) % length
    angles = 2.0 * np.pi * (wave * np.arange(length)[None, :] % length) / length
    return np.cos(angles) + np.sin(angles)


def halves(table):
    high = table.astype(np.float32).astype(BF16)
    return high, (table - high.astype(np.float64)).astype(np.float32).astype(BF16)


def tables():
    second = np.repeat(wave_table(N2, M2).T, N3, axis=1)
    third = np.tile(wave_table(N3, M3).T, (1, N2))
    first = wave_table(N1, M1)
    mixed = np.zeros((N1, 16, HALF, M1))
    for p in range(HALF):
        mixed[:, p, p] = first
    return (
        second.astype(np.float32),
        third.astype(np.float32),
        halves(mixed.reshape(N1 * 16, HALF * M1)),
    )


def ready_kernel(source, vals, val, sems):
    count = 4
    size = MG // count
    copies = []
    for i in range(count):
        where = pl.ds(i * size, size)
        copies.append(pltpu.make_async_copy(source.at[:, where], val.at[:, where], sems.at[i]))
        copies[-1].start()
    for i, copy in enumerate(copies):
        copy.wait()

        def spread(a, carry):
            for t in range(CHUNKS):
                where = pl.ds(pl.multiple_of(a * KP + t * LANES, LANES), LANES)
                vals[pl.ds(t * M1 + a, 16, stride=LINES), :] = val[:, where].astype(F32)
            return carry

        lax.fori_loop(i * M1 // count, (i + 1) * M1 // count, spread, 0)


def ready_call(val, interpret=False):
    return pl.pallas_call(
        ready_kernel,
        out_shape=jax.ShapeDtypeStruct((16 * LINES, LANES), F32),
        in_specs=[pl.BlockSpec(memory_space=pltpu.HBM)],
        out_specs=pl.BlockSpec(memory_space=VMEM),
        scratch_shapes=[VMEM((16, MG), BF16), pltpu.SemaphoreType.DMA((4,))],
        compiler_params=pltpu.CompilerParams(vmem_limit_bytes=12 << 20),
        interpret=interpret,
        name="ready",
    )(stay(val))


def density_kernel(
    place, mine, other, my_count, other_count, vals, *refs,
):
    hbm, refs = refs[:9], refs[9:]
    col_out = refs[0]
    row_outs = refs[1:5]
    cons, lhs, acc, table_a, table_b, done, lines, row_lines = refs[5:13]
    local, sems = refs[13:22], refs[22]
    copies = [pltpu.make_async_copy(a, b, sems.at[i]) for i, (a, b) in enumerate(zip(hbm, local))]
    for copy in copies:
        copy.start()
    con_mine, con_other, second, third, mix_hi, mix_lo, scale, val_e, con_e = local
    band = place[0] >> 7
    z = (place[0] >> 4) & 7
    skip = jnp.where((band == 0) == ((place[0] & 15) < 8), 1, 0)
    for copy in copies[:2]:
        copy.wait()

    def spread(a, carry):
        for t in range(CHUNKS):
            where = pl.ds(pl.multiple_of(a * KP + t * LANES, LANES), LANES)
            line = t * M1 + a
            cons[pl.ds(line, 8, stride=LINES), :] = jnp.concatenate(
                [con_mine[:, where].astype(F32), con_other[:, where].astype(F32)], 0
            )
        return carry

    lax.fori_loop(0, M1, spread, 0)
    for copy in copies[2:]:
        copy.wait()

    is_first = band == 0
    first_count = jnp.where(is_first, my_count[0], other_count[0])
    both_count = my_count[0] + other_count[0]
    lane = lax.broadcasted_iota(jnp.int32, (1, LANES), 1) & 15
    gaps = []
    for h in range(2):
        gap = jnp.ones((1, LANES), F32)
        for p in range(HALF):
            pos = h * HALF + p
            from_first = pos < first_count
            slot = jnp.minimum(jnp.where(from_first, pos, pos - first_count), SLOTS - 1)
            own = from_first == is_first
            v = jnp.where(own, mine[0, slot], other[0, slot])
            c = jnp.where(own, mine[1, slot], other[1, slot])
            gap = jnp.where(lane == p, con_e[c] - val_e[v], gap)
            v_line = v * LINES
            c_line = (jnp.where(own, 0, 4) + (c & 3)) * LINES
            top = pos * M1

            def product(t, carry):
                made = vals[pl.ds(v_line + t * M1, M1), :] * cons[pl.ds(c_line + t * M1, M1), :]
                where = pl.ds(pl.multiple_of(t * LANES, LANES), LANES)
                lhs[top : top + M1, where] = made.astype(BF16)
                return carry

            lax.fori_loop(0, CHUNKS, product, 0, unroll=6)
        gaps.append(gap)

    acc[...] = jnp.zeros_like(acc)

    def make(table, k):
        for i in range(STEP // M3):
            table[i * M3 : (i + 1) * M3, :] = (
                second[pl.ds(k * (STEP // M3) + i, 1), :] * third[...]
            ).astype(BF16)

    def add(table, k):
        where = pl.ds(pl.multiple_of(k * STEP, STEP), STEP)
        acc[...] += jnp.dot(lhs[:, where], table[...], preferred_element_type=F32)

    last = KP // STEP - 1
    make(table_a, 0)

    def transform(k, carry):
        make(table_b, 2 * k + 1)
        add(table_a, 2 * k)
        make(table_a, jnp.minimum(2 * k + 2, last))
        add(table_b, 2 * k + 1)
        return carry

    lax.fori_loop(0, KP // STEP // 2, transform, 0)
    at_lane = lax.broadcasted_iota(jnp.int32, (1, LANES), 1)
    frequency = (at_lane >> 4).astype(F32)
    norm = 1.0 / math.sqrt(MG)
    for h in range(2):
        mid = acc[h * HALF * M1 : (h + 1) * HALF * M1, :]
        mid_hi = mid.astype(BF16)
        mid_lo = (mid - mid_hi.astype(F32)).astype(BF16)
        done[...] = (
            jnp.dot(mix_hi[...], mid_hi, preferred_element_type=F32)
            + jnp.dot(mix_hi[...], mid_lo, preferred_element_type=F32)
            + jnp.dot(mix_lo[...], mid_hi, preferred_element_type=F32)
        )
        gap = gaps[h]
        live = (h * HALF + lane < both_count) & (lane < HALF) & (at_lane < 32)
        weight = jnp.where(
            live, 2.0 * gap / (gap * gap + frequency * frequency), 0.0
        ) * (1.0 / math.sqrt(TOTAL))
        w_hi = weight.astype(BF16).astype(F32)
        w_mid = (weight - w_hi).astype(BF16).astype(F32)
        lines[WIDTH * HALF : WIDTH * HALF + 1, :] = w_hi
        lines[WIDTH * HALF + 1 : WIDTH * HALF + 2, :] = w_mid
        lines[WIDTH * HALF + 2 : WIDTH * HALF + 3, :] = weight - w_hi - w_mid
        lines[WIDTH * HALF + 3 : WIDTH * HALF + 4, :] = jnp.zeros((1, LANES), F32)
        for k in range(N1):
            block = done[k * 16 : (k + 1) * 16, :] * (scale[:, k * NP : (k + 1) * NP] * norm)
            done[k * 16 : (k + 1) * 16, :] = block
            for ch in range(WIDTH):
                lines[ch * HALF : (ch + 1) * HALF, :] = block[:HALF, ch * LANES : (ch + 1) * LANES]
            col_out[k, h] = lines[...].astype(BF16)
        for i in range(4):
            target = jnp.where(band == 0, z + i + skip, z - i - skip + GROW) & 7
            for s in range(2):
                block = done[pl.ds(pl.multiple_of((2 * target + s) * 16, 16), 16), :]
                for ch in range(WIDTH):
                    at = (s * WIDTH + ch) * HALF
                    row_lines[at : at + HALF, :] = block[:HALF, ch * LANES : (ch + 1) * LANES]
            row_outs[i][h] = row_lines[...].astype(BF16)


def stay(array):
    return pltpu.with_memory_space_constraint(jnp.asarray(array), pltpu.HBM)


def density_call(
    place, mine, other, my_count, other_count, val_e, con_e, vals, con_mine, con_other, scale, interpret=False
):
    second, third, (mix_hi, mix_lo) = tables()
    smem = pl.BlockSpec(memory_space=SMEM)
    vmem = pl.BlockSpec(memory_space=VMEM)
    hbm = pl.BlockSpec(memory_space=pltpu.HBM)
    anywhere = pl.BlockSpec(memory_space=pl.ANY)
    return pl.pallas_call(
        density_kernel,
        out_shape=[
            jax.ShapeDtypeStruct((N1, 2, BLOCK, LANES), BF16),
        ]
        + [jax.ShapeDtypeStruct((2, ROWBLOCK, LANES), BF16)] * 4,
        in_specs=[smem] * 5 + [vmem, hbm, anywhere] + [hbm] * 7,
        out_specs=[vmem] * 5,
        scratch_shapes=[
            VMEM((8 * LINES, LANES), F32),
            VMEM((2 * HALF * M1, KP), BF16),
            VMEM((2 * HALF * M1, NP), F32),
            VMEM((STEP, NP), BF16),
            VMEM((STEP, NP), BF16),
            VMEM((N1 * 16, NP), F32),
            VMEM((BLOCK, LANES), F32),
            VMEM((ROWBLOCK, LANES), F32),
            VMEM((4, MG), BF16),
            VMEM((4, MG), BF16),
            VMEM((M2, NP), F32),
            VMEM((M3, NP), F32),
            VMEM((N1 * 16, HALF * M1), BF16),
            VMEM((N1 * 16, HALF * M1), BF16),
            VMEM((1, N1 * NP), F32),
            SMEM((16,), F32),
            SMEM((1024,), F32),
            pltpu.SemaphoreType.DMA((9,)),
        ],
        compiler_params=pltpu.CompilerParams(vmem_limit_bytes=26 << 20),
        interpret=interpret,
        name="density",
    )(place, mine, other, my_count, other_count, vals, stay(con_mine), con_other, stay(second), stay(third),
      stay(mix_hi), stay(mix_lo), stay(scale), stay(val_e), stay(con_e))


def pack_kernel(*refs):
    blocks, out, spread = refs[:4], refs[4], refs[5]
    stride = ROWBLOCK + 4
    for v in range(8):
        spread[v * stride : v * stride + ROWBLOCK, :] = blocks[v // 2][v % 2].astype(F32)
    for ch in range(2 * WIDTH):
        for pp in range(HALF // 2):
            got = [spread[pl.ds(ch * HALF + 2 * pp + q, 8, stride=stride), :] for q in range(2)]
            out[pp * 16 : (pp + 1) * 16, ch * LANES : (ch + 1) * LANES] = jnp.concatenate(
                got, 0
            ).astype(BF16)


def pack_call(blocks, interpret=False):
    vmem = pl.BlockSpec(memory_space=VMEM)
    return pl.pallas_call(
        pack_kernel,
        out_shape=jax.ShapeDtypeStruct((8 * HALF, ROW), BF16),
        in_specs=[vmem] * 4,
        out_specs=vmem,
        scratch_shapes=[VMEM((8 * (ROWBLOCK + 4), LANES), F32)],
        compiler_params=pltpu.CompilerParams(vmem_limit_bytes=4 << 20),
        interpret=interpret,
        name="pack",
    )(*blocks)


def fetch(pieces, rows, sems):
    copies = []
    at = 0
    for i, piece in enumerate(pieces):
        size = piece.shape[0]
        copies.append(pltpu.make_async_copy(piece, rows.at[pl.ds(at, size), :], sems.at[i]))
        copies[-1].start()
        at += size
    return copies


def around(step):
    return jnp.where(step == 0, 0, jnp.where(step == 1, 3, jnp.where(step == 2, 1, 2)))


def assemble_kernel(place, *refs):
    cols = refs[:10]
    away_out, home_out, spread = refs[10:]
    me = place[0]
    band, y, x = me >> 7, (me >> 2) & 3, me & 3

    def take(part, first):
        for i in range(4):
            col = cols[part * 5 + first + i]
            for q in range(GCOL // 2):
                for h in range(2):
                    at = (2 * i + h) * COLROWS + (part * 8 + q) * BLOCK
                    spread[at : at + BLOCK, :] = col[q, h].astype(F32)

    @pl.when(band == 0)
    def _():
        take(0, 1)
        take(1, 0)

    @pl.when(band == 1)
    def _():
        take(0, 0)
        take(1, 1)

    def assemble(j, carry):
        outer, inner = around(j >> 2), around(j & 3)
        dy = jnp.where(band == 0, outer, inner)
        dx = jnp.where(band == 0, inner, outer)
        base = (((y + dy) & 3) * 4 + ((x + dx) & 3)) * BLOCK
        weight = jnp.zeros((GROW, LANES), F32)
        for part in range(3):
            weight += spread[pl.ds(base + WIDTH * HALF + part, GROW, stride=COLROWS), :]
        other = pltpu.roll(weight, LANES - 16, 1)
        away = jnp.where(band == 0, other, weight)
        home = jnp.where(band == 0, weight, other)
        for pp in range(HALF // 2):
            ws = [
                [jnp.broadcast_to(w[:, 2 * pp + q : 2 * pp + q + 1], (GROW, LANES)) for q in range(2)]
                for w in (away, home)
            ]
            to = pl.ds(pl.multiple_of(j * GROW * HALF + pp * 16, 16), 16)
            for ch in range(WIDTH):
                got = [
                    spread[pl.ds(base + ch * HALF + 2 * pp + q, GROW, stride=COLROWS), :]
                    for q in range(2)
                ]
                where = slice(ch * LANES, (ch + 1) * LANES)
                for f, dest in enumerate((away_out, home_out)):
                    dest[to, where] = jnp.concatenate(
                        [got[0] * ws[f][0], got[1] * ws[f][1]], 0
                    ).astype(BF16)
        return carry

    lax.fori_loop(0, GCOL, assemble, 0)


def assemble_call(place, cols, interpret=False):
    vmem = pl.BlockSpec(memory_space=VMEM)
    return pl.pallas_call(
        assemble_kernel,
        out_shape=[jax.ShapeDtypeStruct((PANEL, NP), BF16)] * 2,
        in_specs=[pl.BlockSpec(memory_space=SMEM)] + [vmem] * 10,
        out_specs=[vmem] * 2,
        scratch_shapes=[VMEM((GROW * COLROWS, LANES), F32)],
        compiler_params=pltpu.CompilerParams(vmem_limit_bytes=14 << 20),
        interpret=interpret,
        name="assemble",
    )(place, *cols)


PIECES = 8


def away_kernel(weighted, *refs):
    pieces = refs[:PIECES]
    away_out, turned_out, rows, sems = refs[PIECES:]
    for copy in fetch(pieces, rows, sems):
        copy.wait()

    def product(m, carry):
        where = pl.ds(pl.multiple_of(m * 256, 256), 256)
        part = rows[:, where].T
        turned_out[where, :] = part
        away_out[where, :] = jnp.dot(part, weighted[...], preferred_element_type=F32).astype(BF16)
        return carry

    lax.fori_loop(0, ROW // 256, product, 0)


def away_call(weighted, pieces, interpret=False):
    vmem = pl.BlockSpec(memory_space=VMEM)
    return pl.pallas_call(
        away_kernel,
        out_shape=(
            jax.ShapeDtypeStruct((ROW, NP), BF16),
            jax.ShapeDtypeStruct((ROW, PANEL), BF16),
        ),
        in_specs=[vmem] + [pl.BlockSpec(memory_space=pl.ANY)] * PIECES,
        out_specs=(vmem, vmem),
        scratch_shapes=[VMEM((PANEL, ROW), BF16), pltpu.SemaphoreType.DMA((PIECES,))],
        compiler_params=pltpu.CompilerParams(vmem_limit_bytes=20 << 20),
        interpret=interpret,
        name="away",
    )(weighted, *pieces)


def home_kernel(weighted, rows, home_out):
    def product(m, carry):
        where = pl.ds(pl.multiple_of(m * 256, 256), 256)
        home_out[where, :] = jnp.dot(rows[where, :], weighted[...], preferred_element_type=F32)
        return carry

    lax.fori_loop(0, ROW // 256, product, 0)


def home_call(weighted, rows, interpret=False):
    vmem = pl.BlockSpec(memory_space=VMEM)
    return pl.pallas_call(
        home_kernel,
        out_shape=jax.ShapeDtypeStruct((ROW, NP), F32),
        in_specs=[vmem, vmem],
        out_specs=vmem,
        compiler_params=pltpu.CompilerParams(vmem_limit_bytes=16 << 20),
        interpret=interpret,
        name="home",
    )(weighted, rows)


PLANE = ("band", "gcol_0", "gcol_1")


def turned(array, phase, step):
    pairs = []
    for band in range(2):
        along_x = (band == 0) == (phase == 0)
        for y in range(4):
            for x in range(4):
                to = (y, (x + step) % 4) if along_x else ((y + step) % 4, x)
                pairs.append((band * 16 + y * 4 + x, band * 16 + to[0] * 4 + to[1]))
    return lax.ppermute(array, PLANE, pairs)


ALL = ("band", "grow", "gcol_0", "gcol_1")


def along(array, steps):
    pairs = []
    for band in range(2):
        for plane in range(GCOL):
            step = steps((band == 0) == (plane < 8), band)
            if step is None:
                continue
            for z in range(GROW):
                to = (z + step) % GROW if band == 0 else (z - step) % GROW
                pairs.append(((band * GROW + z) * GCOL + plane, (band * GROW + to) * GCOL + plane))
    return lax.ppermute(array, ALL, pairs)


def swap(array):
    return lax.ppermute(array, "band", [(0, 1), (1, 0)])


def per_device(
    valence_orbitals,
    conduction_orbitals,
    valence_energy,
    conduction_energy,
    coulomb_root,
    pair_bands,
    slot_counts,
):
    place = lax.axis_index(("band", "grow", "gcol_0", "gcol_1")).astype(jnp.int32).reshape(1)
    other_con = swap(conduction_orbitals)
    other_pairs, other_count = swap(pair_bands), swap(slot_counts)
    vals = ready_call(valence_orbitals)
    col, *rows = density_call(
        place, pair_bands, other_pairs, slot_counts, other_count, valence_energy, conduction_energy,
        vals, conduction_orbitals, other_con, coulomb_root.reshape(1, N1 * NP),
    )
    return exchange(place, col, rows)


def exchange(place, col, rows):
    rows = [along(rows[i], lambda f, b, i=i: i + 1 if f else i) for i in range(4)]
    col = lax.all_to_all(col, ("gcol_0", "gcol_1"), 0, 0, tiled=True)
    row = pack_call(rows)
    parts = [col[:8], col[8:]]
    rings = []
    for part in range(2):
        ring = [parts[part]]
        for i in range(1, 5):
            ring.append(
                along(ring[-1], lambda f, b, i=i, part=part: 1 if i < 4 or b == part else None)
            )
        rings += ring
    half = row.shape[0] // 2
    below, above = turned(row, 0, 1), turned(row, 0, -1)
    far_a, far_b = turned(below[:half], 0, 1), turned(above[half:], 0, -1)
    first = jnp.concatenate([row, below], 0)
    second = jnp.concatenate([above, far_a, far_b], 0)
    below_a, above_a = turned(first, 1, 1), turned(first, 1, -1)
    above_b, below_b = turned(second, 1, -1), turned(second, 1, 1)
    far_a, far_b = turned(below_a, 1, 1), turned(above_b, 1, -1)
    weighted_away, weighted_home = assemble_call(place, rings)
    pieces = [first, second, below_a, below_b, above_a, above_b, far_a, far_b]
    away, turned_rows = away_call(weighted_away, pieces)
    received = swap(away)
    home = home_call(weighted_home, turned_rows)
    return -(home + received.astype(F32))[None]


def solution(mesh):
    finer = Mesh(
        mesh.devices.reshape(mesh.shape["band"], mesh.shape["grow"], 4, 4),
        ("band", "grow", "gcol_0", "gcol_1"),
    )
    everywhere = ("band", "grow", "gcol_0", "gcol_1")
    in_specs = (P(), P(everywhere, None), P(), P(), P(), P(None, everywhere), P(everywhere))
    return jax.shard_map(
        per_device,
        mesh=finer,
        in_specs=in_specs,
        out_specs=P("band", "grow", ("gcol_0", "gcol_1")),
        check_vma=False,
    )
```

profile of v0, /device:TPU:1, one launch (start us, length us, event | category | flops | bytes accessed | tf_op | source)
XLA Modules:
  0.0 111.5 jit_solution(10019144434357138561)
XLA Ops:
  0.0 3.2 %collective-permute-start.2 = (bf16[4,98304]{1,0:T(4,128)(2,1)}, bf16[4,98304]{1,0:T(4,128)(2,1)S(1)}, u32[]{:S(2)}, u32[]{:S(2)}) collective-permute-start(bf16[4,98304]{1,0:T(4,128)(2,1)} %refs_0_.1), channel_id=1, source_target_pairs={{0,128},{128,0},{1,129},{129,1},{2,130},{130,2},{3,131},{131,3},{4... | collective-permute-start | bytes 2359304 | tf_op jit(solution)/shard_map/ppermute | solution.py:464
  3.2 0.0 collective-permute-start.1
  3.2 0.5 collective-permute-start
  4.4 0.0 copy-start.2
  4.4 2.1 %ready.1.vals = f32[12352,128]{1,0:T(8,128)S(1)} custom-call(bf16[16,98304]{1,0:T(8,128)(2,1)} %source.1), custom_call_target="tpu_custom_call" | custom-call | tf_op jit(solution)/shard_map/ready/pallas_call | solution.py:83
  6.5 2.6 %copy-done = f32[12352,128]{1,0:T(8,128)} copy-done((f32[12352,128]{1,0:T(8,128)}, f32[12352,128]{1,0:T(8,128)S(1)}, u32[]{:S(2)}) %copy-start) | copy-done | bytes 6324248
  9.2 0.0 collective-permute-done.1.other_count
  9.2 0.0 collective-permute-done.other
  9.2 0.0 collective-permute-done.2.refs_1_
  9.2 2.8 %copy-done.1 = f32[12352,128]{1,0:T(8,128)S(1)} copy-done((f32[12352,128]{1,0:T(8,128)S(1)}, f32[12352,128]{1,0:T(8,128)}, u32[]{:S(2)}) %copy-start.1) | copy-done | bytes 6324248
  12.0 12.7 %density.1 = (bf16[16,2,64,128]{3,2,1,0:T(8,128)(2,1)}, bf16[2,120,128]{2,1,0:T(8,128)(2,1)S(1)}, bf16[2,120,128]{2,1,0:T(8,128)(2,1)S(1)}, bf16[2,120,128]{2,1,0:T(8,128)(2,1)S(1)}, bf16[2,120,128]{2,1,0:T(8,128)(2,1)S(1)}) custom-call(s32[1]{0:T(128)} %bitcast.place, s32[2,20]{1,0:T(2,128)S(1)} %copy-done.2, s32[2,20]{1,0:T(2,128)S(1)} %collective-permute-done.other, ...), custom_call_target="tpu_custom_call" | custom-call | tf_op jit(solution)/shard_map/density/pallas_call | solution.py:228
  24.7 0.7 collective-permute-start.11
  25.4 3.9 %collective-permute-start.12 = (bf16[2,120,128]{2,1,0:T(8,128)(2,1)S(1)}, bf16[2,120,128]{2,1,0:T(8,128)(2,1)S(1)}, u32[]{:S(2)}, u32[]{:S(2)}) collective-permute-start(bf16[2,120,128]{2,1,0:T(8,128)(2,1)S(1)} %get-tuple-element.18), channel_id=1, source_target_pairs={{0,32},{16,48},{32,64},{48,80},{64,96},{80,112},{96,0},{112,16},{1... | collective-permute-start | bytes 184328 | tf_op jit(solution)/shard_map/ppermute | solution.py:460
  29.4 1.2 %collective-permute-start.13 = (bf16[2,120,128]{2,1,0:T(8,128)(2,1)S(1)}, bf16[2,120,128]{2,1,0:T(8,128)(2,1)S(1)}, u32[]{:S(2)}, u32[]{:S(2)}) collective-permute-start(bf16[2,120,128]{2,1,0:T(8,128)(2,1)S(1)} %get-tuple-element.19), channel_id=1, source_target_pairs={{0,48},{16,64},{32,80},{48,96},{64,112},{80,0},{96,16},{112,32},{1... | collective-permute-start | bytes 184328 | tf_op jit(solution)/shard_map/ppermute | solution.py:460
  30.5 0.4 collective-permute-start.14
  31.0 12.5 %all-to-all-start = ((bf16[16,2,64,128]{3,2,1,0:T(8,128)(2,1)}), bf16[16,2,64,128]{3,2,1,0:T(8,128)(2,1)S(1)}, u32[]{:S(2)}, u32[]{:S(2)}) async-start(bf16[16,2,64,128]{3,2,1,0:T(8,128)(2,1)} %get-tuple-element.14), calls=%async_computation | async-start | bytes 1048576 | tf_op jit(solution)/shard_map/all_to_all | solution.py:489
  43.5 0.0 collective-permute-done.11.refs_0_
  43.5 0.0 collective-permute-done.12.refs_1_
  43.5 0.0 collective-permute-done.13.refs_2_
  43.5 0.0 collective-permute-done.14.refs_3_
  43.5 0.1 pack.1
  43.6 2.7 %collective-permute-start.16 = (bf16[80,1536]{1,0:T(8,128)(2,1)S(1)}, bf16[80,1536]{1,0:T(8,128)(2,1)S(1)}, u32[]{:S(2)}, u32[]{:S(2)}) collective-permute-start(bf16[80,1536]{1,0:T(8,128)(2,1)S(1)} %pack.1), channel_id=1, source_target_pairs={{0,3},{1,0},{2,1},{3,2},{4,7},{5,4},{6,5},{7,6},{8,11},{9,8},{10,9... | collective-permute-start | bytes 737288 | tf_op jit(solution)/shard_map/ppermute | solution.py:444
  46.3 0.0 collective-permute-start.15
  46.3 7.0 %collective-permute-done.16 = bf16[80,1536]{1,0:T(8,128)(2,1)S(1)} collective-permute-done((bf16[80,1536]{1,0:T(8,128)(2,1)S(1)}, bf16[80,1536]{1,0:T(8,128)(2,1)S(1)}, u32[]{:S(2)}, u32[]{:S(2)}) %collective-permute-start.16) | collective-permute-done | bytes 245792 | tf_op jit(solution)/shard_map/ppermute | solution.py:444
  53.3 2.0 %collective-permute-start.18 = (bf16[40,1536]{1,0:T(8,128)(2,1)S(1)}, bf16[40,1536]{1,0:T(8,128)(2,1)S(1)}, u32[]{:S(2)}, u32[]{:S(2)}) collective-permute-start(bf16[40,1536]{1,0:T(8,128)(2,1)S(1)} %slice.19), channel_id=1, source_target_pairs={{0,3},{1,0},{2,1},{3,2},{4,7},{5,4},{6,5},{7,6},{8,11},{9,8},{10,9... | collective-permute-start | bytes 368648 | tf_op jit(solution)/shard_map/ppermute | solution.py:444
  55.3 0.0 collective-permute-done.15
  55.3 0.3 collective-permute-start.17
  55.6 0.4 collective-permute-start.19
  56.0 0.0 all-to-all-done
  56.1 2.0 %collective-permute-start.7 = (bf16[8,2,64,128]{3,2,1,0:T(8,128)(2,1)S(1)}, bf16[8,2,64,128]{3,2,1,0:T(8,128)(2,1)S(1)}, u32[]{:S(2)}, u32[]{:S(2)}) collective-permute-start(bf16[8,2,64,128]{3,2,1,0:T(8,128)(2,1)S(1)} %get-tuple-element.23.refs_5_), channel_id=1, source_target_pairs={{0,16},{16,32},{32,48},{48,64},{64,80},{80,96},{96,112},{112,0},{1... | collective-permute-start | bytes 786440 | tf_op jit(solution)/shard_map/ppermute | solution.py:460
  58.1 0.8 collective-permute-start.3
  58.9 3.2 %collective-permute-done.17 = bf16[40,1536]{1,0:T(8,128)(2,1)S(1)} collective-permute-done((bf16[40,1536]{1,0:T(8,128)(2,1)S(1)}, bf16[40,1536]{1,0:T(8,128)(2,1)S(1)}, u32[]{:S(2)}, u32[]{:S(2)}) %collective-permute-start.17) | collective-permute-done | bytes 122912 | tf_op jit(solution)/shard_map/ppermute | solution.py:444
  62.1 0.0 collective-permute-done.7.refs_6_
  62.1 2.7 %collective-permute-start.8 = (bf16[8,2,64,128]{3,2,1,0:T(8,128)(2,1)S(1)}, bf16[8,2,64,128]{3,2,1,0:T(8,128)(2,1)S(1)}, u32[]{:S(2)}, u32[]{:S(2)}) collective-permute-start(bf16[8,2,64,128]{3,2,1,0:T(8,128)(2,1)S(1)} %collective-permute-done.7.refs_6_), channel_id=1, source_target_pairs={{0,16},{16,32},{32,48},{48,64},{64,80},{80,96},{96,112},{112,0},{1... | collective-permute-start | bytes 786440 | tf_op jit(solution)/shard_map/ppermute | solution.py:460
  64.8 0.0 collective-permute-done.3.refs_1_
  64.8 2.8 %collective-permute-start.4 = (bf16[8,2,64,128]{3,2,1,0:T(8,128)(2,1)S(1)}, bf16[8,2,64,128]{3,2,1,0:T(8,128)(2,1)S(1)}, u32[]{:S(2)}, u32[]{:S(2)}) collective-permute-start(bf16[8,2,64,128]{3,2,1,0:T(8,128)(2,1)S(1)} %collective-permute-done.3.refs_1_), channel_id=1, source_target_pairs={{0,16},{16,32},{32,48},{48,64},{64,80},{80,96},{96,112},{112,0},{1... | collective-permute-start | bytes 786440 | tf_op jit(solution)/shard_map/ppermute | solution.py:460
  67.6 0.0 collective-permute-done.18
  67.6 2.3 %collective-permute-start.22 = (bf16[160,1536]{1,0:T(8,128)(2,1)S(1)}, bf16[160,1536]{1,0:T(8,128)(2,1)S(1)}, u32[]{:S(2)}, u32[]{:S(2)}) collective-permute-start(bf16[160,1536]{1,0:T(8,128)(2,1)S(1)} %constant_dynamic-update-slice_fusion.refs_1_), channel_id=1, source_target_pairs={{0,12},{1,13},{2,14},{3,15},{4,0},{5,1},{6,2},{7,3},{8,4},{9,5},{1... | collective-permute-start | bytes 1474568 | tf_op jit(solution)/shard_map/ppermute | solution.py:444
  69.9 0.0 collective-permute-done.8.refs_7_
  69.9 1.3 %collective-permute-start.9 = (bf16[8,2,64,128]{3,2,1,0:T(8,128)(2,1)S(1)}, bf16[8,2,64,128]{3,2,1,0:T(8,128)(2,1)S(1)}, u32[]{:S(2)}, u32[]{:S(2)}) collective-permute-start(bf16[8,2,64,128]{3,2,1,0:T(8,128)(2,1)S(1)} %collective-permute-done.8.refs_7_), channel_id=1, source_target_pairs={{0,16},{16,32},{32,48},{48,64},{64,80},{80,96},{96,112},{112,0},{1... | collective-permute-start | bytes 786440 | tf_op jit(solution)/shard_map/ppermute | solution.py:460
  71.2 0.0 collective-permute-done.4.refs_2_
  71.2 2.8 %collective-permute-start.5 = (bf16[8,2,64,128]{3,2,1,0:T(8,128)(2,1)S(1)}, bf16[8,2,64,128]{3,2,1,0:T(8,128)(2,1)S(1)}, u32[]{:S(2)}, u32[]{:S(2)}) collective-permute-start(bf16[8,2,64,128]{3,2,1,0:T(8,128)(2,1)S(1)} %collective-permute-done.4.refs_2_), channel_id=1, source_target_pairs={{0,16},{16,32},{32,48},{48,64},{64,80},{80,96},{96,112},{112,0},{1... | collective-permute-start | bytes 786440 | tf_op jit(solution)/shard_map/ppermute | solution.py:460
  74.0 1.4 %collective-permute-done.9.refs_8_ = bf16[8,2,64,128]{3,2,1,0:T(8,128)(2,1)S(1)} collective-permute-done((bf16[8,2,64,128]{3,2,1,0:T(8,128)(2,1)S(1)}, bf16[8,2,64,128]{3,2,1,0:T(8,128)(2,1)S(1)}, u32[]{:S(2)}, u32[]{:S(2)}) %collective-permute-start.9) | collective-permute-done | bytes 262176 | tf_op jit(solution)/shard_map/ppermute | solution.py:460
  75.4 4.1 %collective-permute-start.10 = (bf16[8,2,64,128]{3,2,1,0:T(8,128)(2,1)S(1)}, bf16[8,2,64,128]{3,2,1,0:T(8,128)(2,1)S(1)}, u32[]{:S(2)}, u32[]{:S(2)}) collective-permute-start(bf16[8,2,64,128]{3,2,1,0:T(8,128)(2,1)S(1)} %collective-permute-done.9.refs_8_), channel_id=1, source_target_pairs={{128,240},{144,128},{160,144},{176,160},{192,176},{208,192},{224,2... | collective-permute-start | bytes 786440 | tf_op jit(solution)/shard_map/ppermute | solution.py:460
  79.6 2.6 %collective-permute-start.21 = (bf16[160,1536]{1,0:T(8,128)(2,1)S(1)}, bf16[160,1536]{1,0:T(8,128)(2,1)S(1)}, u32[]{:S(2)}, u32[]{:S(2)}) collective-permute-start(bf16[160,1536]{1,0:T(8,128)(2,1)S(1)} %pad_maximum_fusion.refs_0_), channel_id=1, source_target_pairs={{0,12},{1,13},{2,14},{3,15},{4,0},{5,1},{6,2},{7,3},{8,4},{9,5},{1... | collective-permute-start | bytes 1474568 | tf_op jit(solution)/shard_map/ppermute | solution.py:444
  82.2 0.0 collective-permute-done.19.refs_2_
  82.2 0.0 collective-permute-start.20
  82.2 0.0 collective-permute-done.22.refs_5_
  82.2 0.1 collective-permute-start.23
  82.3 0.0 collective-permute-done.5.refs_3_
  82.3 2.7 %collective-permute-start.24 = (bf16[160,1536]{1,0:T(8,128)(2,1)S(1)}, bf16[160,1536]{1,0:T(8,128)(2,1)S(1)}, u32[]{:S(2)}, u32[]{:S(2)}) collective-permute-start(bf16[160,1536]{1,0:T(8,128)(2,1)S(1)} %collective-permute-done.22.refs_5_), channel_id=1, source_target_pairs={{0,12},{1,13},{2,14},{3,15},{4,0},{5,1},{6,2},{7,3},{8,4},{9,5},{1... | collective-permute-start | bytes 1474568 | tf_op jit(solution)/shard_map/ppermute | solution.py:444
  84.9 0.0 collective-permute-done.10.refs_9_
  84.9 0.7 collective-permute-start.6
  85.6 0.0 collective-permute-done.6.refs_4_
  85.6 3.2 %assemble.1 = (bf16[1280,768]{1,0:T(8,128)(2,1)S(1)}, bf16[1280,768]{1,0:T(8,128)(2,1)S(1)}) custom-call(s32[1]{0:T(128)} %bitcast.place, bf16[8,2,64,128]{3,2,1,0:T(8,128)(2,1)S(1)} %get-tuple-element.24.refs_0_, bf16[8,2,64,128]{3,2,1,0:T(8,128)(2,1)S(1)} %collective-permute-done.3.refs_1_, bf16[8,2,64,128]{3,2,1,0:T(8,128)(2,1)S(1)} %collective-permute-done.4.refs_2_, ...), custom_call_target="tpu_custom_call" | custom-call | tf_op jit(solution)/shard_map/assemble/pallas_call | solution.py:363
  88.8 0.0 collective-permute-done.21.refs_4_
  88.9 2.5 %collective-permute-done.20.refs_3_ = bf16[160,1536]{1,0:T(8,128)(2,1)S(1)} collective-permute-done((bf16[160,1536]{1,0:T(8,128)(2,1)S(1)}, bf16[160,1536]{1,0:T(8,128)(2,1)S(1)}, u32[]{:S(2)}, u32[]{:S(2)}) %collective-permute-start.20) | collective-permute-done | bytes 491552 | tf_op jit(solution)/shard_map/ppermute | solution.py:444
  91.3 5.0 %collective-permute-done.23.refs_6_ = bf16[160,1536]{1,0:T(8,128)(2,1)S(1)} collective-permute-done((bf16[160,1536]{1,0:T(8,128)(2,1)S(1)}, bf16[160,1536]{1,0:T(8,128)(2,1)S(1)}, u32[]{:S(2)}, u32[]{:S(2)}) %collective-permute-start.23) | collective-permute-done | bytes 491552 | tf_op jit(solution)/shard_map/ppermute | solution.py:444
  96.3 0.0 collective-permute-done.24.refs_7_
  96.3 6.9 %away.1 = (bf16[1536,768]{1,0:T(8,128)(2,1)S(1)}, bf16[1536,1280]{1,0:T(8,128)(2,1)S(1)}) custom-call(bf16[1280,768]{1,0:T(8,128)(2,1)S(1)} %get-tuple-element.16.weighted, bf16[160,1536]{1,0:T(8,128)(2,1)S(1)} %pad_maximum_fusion.refs_0_, bf16[160,1536]{1,0:T(8,128)(2,1)S(1)} %constant_dynamic-update-slice_fusion.refs_1_, ...), custom_call_target="tpu_custom_call" | custom-call | tf_op jit(solution)/shard_map/away/pallas_call | solution.py:396
  103.3 1.4 %collective-permute-start.25 = (bf16[1536,768]{1,0:T(8,128)(2,1)S(1)}, bf16[1536,768]{1,0:T(8,128)(2,1)S(1)}, u32[]{:S(2)}, u32[]{:S(2)}) collective-permute-start(bf16[1536,768]{1,0:T(8,128)(2,1)S(1)} %get-tuple-element.22), channel_id=1, source_target_pairs={{0,128},{128,0},{1,129},{129,1},{2,130},{130,2},{3,131},{131,3},{4... | collective-permute-start | bytes 7077896 | tf_op jit(solution)/shard_map/ppermute | solution.py:464
  104.7 4.1 %home.1 = f32[1536,768]{1,0:T(8,128)S(1)} custom-call(bf16[1280,768]{1,0:T(8,128)(2,1)S(1)} %get-tuple-element.15.weighted, bf16[1536,1280]{1,0:T(8,128)(2,1)S(1)} %get-tuple-element.21.rows), custom_call_target="tpu_custom_call" | custom-call | tf_op jit(solution)/shard_map/home/pallas_call | solution.py:422
  108.8 0.1 collective-permute-done.25
  108.9 2.6 %negate_bitcast_fusion = f32[1,1536,768]{2,1,0:T(8,128)} fusion(f32[1536,768]{1,0:T(8,128)S(1)} %home.1, bf16[1536,768]{1,0:T(8,128)(2,1)S(1)} %collective-permute-done.25), kind=kLoop, calls=%fused_computation | loop fusion | flops 3538944 | bytes 11796480 | tf_op jit(solution)/shard_map/neg | solution.py:513
  (10 shorter events, 0.1 us)
Async XLA Ops:
  0.0 9.2 %collective-permute-start.2 = (bf16[4,98304]{1,0:T(4,128)(2,1)}, bf16[4,98304]{1,0:T(4,128)(2,1)S(1)}, u32[]{:S(2)}, u32[]{:S(2)}) collective-permute-start(bf16[4,98304]{1,0:T(4,128)(2,1)} %refs_0_.1), channel_id=1, source_target_pairs={{0,128},{128,0},{1,129},{129,1},{2,130},{130,2},{3,131},{131,3},{4... | collective-permute-start | bytes 2359304 | tf_op jit(solution)/shard_map/ppermute | solution.py:464
  3.2 6.0 %collective-permute-start.1 = (s32[1]{0:T(128)}, s32[1]{0:T(128)}, u32[]{:S(2)}, u32[]{:S(2)}) collective-permute-start(s32[1]{0:T(128)} %param.17), channel_id=1, source_target_pairs={{0,128},{128,0},{1,129},{129,1},{2,130},{130,2},{3,131},{131,3},{4... | collective-permute-start | bytes 20 | tf_op jit(solution)/shard_map/ppermute | solution.py:464
  3.2 6.0 %collective-permute-start = (s32[2,20]{1,0:T(2,128)}, s32[2,20]{1,0:T(2,128)S(1)}, u32[]{:S(2)}, u32[]{:S(2)}) collective-permute-start(s32[2,20]{1,0:T(2,128)} %mine.1), channel_id=1, source_target_pairs={{0,128},{128,0},{1,129},{129,1},{2,130},{130,2},{3,131},{131,3},{4... | collective-permute-start | bytes 488 | tf_op jit(solution)/shard_map/ppermute | solution.py:464
  4.4 4.8 %copy-start.2 = (s32[2,20]{1,0:T(2,128)S(1)}, s32[2,20]{1,0:T(2,128)}, u32[]{:S(2)}) copy-start(s32[2,20]{1,0:T(2,128)} %mine.1) | copy-start | bytes 484
  6.5 2.6 %copy-start = (f32[12352,128]{1,0:T(8,128)}, f32[12352,128]{1,0:T(8,128)S(1)}, u32[]{:S(2)}) copy-start(f32[12352,128]{1,0:T(8,128)S(1)} %ready.1.vals) | copy-start | bytes 18972676
  9.2 2.8 %copy-start.1 = (f32[12352,128]{1,0:T(8,128)S(1)}, f32[12352,128]{1,0:T(8,128)}, u32[]{:S(2)}) copy-start(f32[12352,128]{1,0:T(8,128)} %copy-done) | copy-start | bytes 18972676
  24.7 18.7 %collective-permute-start.11 = (bf16[2,120,128]{2,1,0:T(8,128)(2,1)S(1)}, bf16[2,120,128]{2,1,0:T(8,128)(2,1)S(1)}, u32[]{:S(2)}, u32[]{:S(2)}) collective-permute-start(bf16[2,120,128]{2,1,0:T(8,128)(2,1)S(1)} %get-tuple-element.17), channel_id=1, source_target_pairs={{0,16},{16,32},{32,48},{48,64},{64,80},{80,96},{96,112},{112,0},{1... | collective-permute-start | bytes 184328 | tf_op jit(solution)/shard_map/ppermute | solution.py:460
  25.4 18.1 %collective-permute-start.12 = (bf16[2,120,128]{2,1,0:T(8,128)(2,1)S(1)}, bf16[2,120,128]{2,1,0:T(8,128)(2,1)S(1)}, u32[]{:S(2)}, u32[]{:S(2)}) collective-permute-start(bf16[2,120,128]{2,1,0:T(8,128)(2,1)S(1)} %get-tuple-element.18), channel_id=1, source_target_pairs={{0,32},{16,48},{32,64},{48,80},{64,96},{80,112},{96,0},{112,16},{1... | collective-permute-start | bytes 184328 | tf_op jit(solution)/shard_map/ppermute | solution.py:460
  29.4 14.1 %collective-permute-start.13 = (bf16[2,120,128]{2,1,0:T(8,128)(2,1)S(1)}, bf16[2,120,128]{2,1,0:T(8,128)(2,1)S(1)}, u32[]{:S(2)}, u32[]{:S(2)}) collective-permute-start(bf16[2,120,128]{2,1,0:T(8,128)(2,1)S(1)} %get-tuple-element.19), channel_id=1, source_target_pairs={{0,48},{16,64},{32,80},{48,96},{64,112},{80,0},{96,16},{112,32},{1... | collective-permute-start | bytes 184328 | tf_op jit(solution)/shard_map/ppermute | solution.py:460
  30.5 13.0 %collective-permute-start.14 = (bf16[2,120,128]{2,1,0:T(8,128)(2,1)S(1)}, bf16[2,120,128]{2,1,0:T(8,128)(2,1)S(1)}, u32[]{:S(2)}, u32[]{:S(2)}) collective-permute-start(bf16[2,120,128]{2,1,0:T(8,128)(2,1)S(1)} %get-tuple-element.20), channel_id=1, source_target_pairs={{0,64},{16,80},{32,96},{48,112},{64,0},{80,16},{96,32},{112,48},{1... | collective-permute-start | bytes 184328 | tf_op jit(solution)/shard_map/ppermute | solution.py:460
  31.0 25.1 %all-to-all-start = ((bf16[16,2,64,128]{3,2,1,0:T(8,128)(2,1)}), bf16[16,2,64,128]{3,2,1,0:T(8,128)(2,1)S(1)}, u32[]{:S(2)}, u32[]{:S(2)}) async-start(bf16[16,2,64,128]{3,2,1,0:T(8,128)(2,1)} %get-tuple-element.14), calls=%async_computation | async-start | bytes 1048576 | tf_op jit(solution)/shard_map/all_to_all | solution.py:489
  43.6 9.7 %collective-permute-start.16 = (bf16[80,1536]{1,0:T(8,128)(2,1)S(1)}, bf16[80,1536]{1,0:T(8,128)(2,1)S(1)}, u32[]{:S(2)}, u32[]{:S(2)}) collective-permute-start(bf16[80,1536]{1,0:T(8,128)(2,1)S(1)} %pack.1), channel_id=1, source_target_pairs={{0,3},{1,0},{2,1},{3,2},{4,7},{5,4},{6,5},{7,6},{8,11},{9,8},{10,9... | collective-permute-start | bytes 737288 | tf_op jit(solution)/shard_map/ppermute | solution.py:444
  46.3 9.0 %collective-permute-start.15 = (bf16[80,1536]{1,0:T(8,128)(2,1)S(1)}, bf16[80,1536]{1,0:T(8,128)(2,1)S(1)}, u32[]{:S(2)}, u32[]{:S(2)}) collective-permute-start(bf16[80,1536]{1,0:T(8,128)(2,1)S(1)} %pack.1), channel_id=1, source_target_pairs={{0,1},{1,2},{2,3},{3,0},{4,5},{5,6},{6,7},{7,4},{8,9},{9,10},{10,1... | collective-permute-start | bytes 737288 | tf_op jit(solution)/shard_map/ppermute | solution.py:444
  53.3 14.3 %collective-permute-start.18 = (bf16[40,1536]{1,0:T(8,128)(2,1)S(1)}, bf16[40,1536]{1,0:T(8,128)(2,1)S(1)}, u32[]{:S(2)}, u32[]{:S(2)}) collective-permute-start(bf16[40,1536]{1,0:T(8,128)(2,1)S(1)} %slice.19), channel_id=1, source_target_pairs={{0,3},{1,0},{2,1},{3,2},{4,7},{5,4},{6,5},{7,6},{8,11},{9,8},{10,9... | collective-permute-start | bytes 368648 | tf_op jit(solution)/shard_map/ppermute | solution.py:444
  55.3 6.8 %collective-permute-start.17 = (bf16[40,1536]{1,0:T(8,128)(2,1)S(1)}, bf16[40,1536]{1,0:T(8,128)(2,1)S(1)}, u32[]{:S(2)}, u32[]{:S(2)}) collective-permute-start(bf16[40,1536]{1,0:T(8,128)(2,1)S(1)} %slice.18), channel_id=1, source_target_pairs={{0,1},{1,2},{2,3},{3,0},{4,5},{5,6},{6,7},{7,4},{8,9},{9,10},{10,1... | collective-permute-start | bytes 368648 | tf_op jit(solution)/shard_map/ppermute | solution.py:444
  55.6 26.6 %collective-permute-start.19 = (bf16[160,1536]{1,0:T(8,128)(2,1)S(1)}, bf16[160,1536]{1,0:T(8,128)(2,1)S(1)}, u32[]{:S(2)}, u32[]{:S(2)}) collective-permute-start(bf16[160,1536]{1,0:T(8,128)(2,1)S(1)} %pad_maximum_fusion.refs_0_), channel_id=1, source_target_pairs={{0,4},{1,5},{2,6},{3,7},{4,8},{5,9},{6,10},{7,11},{8,12},{9,13},{1... | collective-permute-start | bytes 1474568 | tf_op jit(solution)/shard_map/ppermute | solution.py:444
  56.1 6.0 %collective-permute-start.7 = (bf16[8,2,64,128]{3,2,1,0:T(8,128)(2,1)S(1)}, bf16[8,2,64,128]{3,2,1,0:T(8,128)(2,1)S(1)}, u32[]{:S(2)}, u32[]{:S(2)}) collective-permute-start(bf16[8,2,64,128]{3,2,1,0:T(8,128)(2,1)S(1)} %get-tuple-element.23.refs_5_), channel_id=1, source_target_pairs={{0,16},{16,32},{32,48},{48,64},{64,80},{80,96},{96,112},{112,0},{1... | collective-permute-start | bytes 786440 | tf_op jit(solution)/shard_map/ppermute | solution.py:460
  58.1 6.7 %collective-permute-start.3 = (bf16[8,2,64,128]{3,2,1,0:T(8,128)(2,1)S(1)}, bf16[8,2,64,128]{3,2,1,0:T(8,128)(2,1)S(1)}, u32[]{:S(2)}, u32[]{:S(2)}) collective-permute-start(bf16[8,2,64,128]{3,2,1,0:T(8,128)(2,1)S(1)} %get-tuple-element.24.refs_0_), channel_id=1, source_target_pairs={{0,16},{16,32},{32,48},{48,64},{64,80},{80,96},{96,112},{112,0},{1... | collective-permute-start | bytes 786440 | tf_op jit(solution)/shard_map/ppermute | solution.py:460
  62.1 7.8 %collective-permute-start.8 = (bf16[8,2,64,128]{3,2,1,0:T(8,128)(2,1)S(1)}, bf16[8,2,64,128]{3,2,1,0:T(8,128)(2,1)S(1)}, u32[]{:S(2)}, u32[]{:S(2)}) collective-permute-start(bf16[8,2,64,128]{3,2,1,0:T(8,128)(2,1)S(1)} %collective-permute-done.7.refs_6_), channel_id=1, source_target_pairs={{0,16},{16,32},{32,48},{48,64},{64,80},{80,96},{96,112},{112,0},{1... | collective-permute-start | bytes 786440 | tf_op jit(solution)/shard_map/ppermute | solution.py:460
  64.8 6.4 %collective-permute-start.4 = (bf16[8,2,64,128]{3,2,1,0:T(8,128)(2,1)S(1)}, bf16[8,2,64,128]{3,2,1,0:T(8,128)(2,1)S(1)}, u32[]{:S(2)}, u32[]{:S(2)}) collective-permute-start(bf16[8,2,64,128]{3,2,1,0:T(8,128)(2,1)S(1)} %collective-permute-done.3.refs_1_), channel_id=1, source_target_pairs={{0,16},{16,32},{32,48},{48,64},{64,80},{80,96},{96,112},{112,0},{1... | collective-permute-start | bytes 786440 | tf_op jit(solution)/shard_map/ppermute | solution.py:460
  67.6 14.6 %collective-permute-start.22 = (bf16[160,1536]{1,0:T(8,128)(2,1)S(1)}, bf16[160,1536]{1,0:T(8,128)(2,1)S(1)}, u32[]{:S(2)}, u32[]{:S(2)}) collective-permute-start(bf16[160,1536]{1,0:T(8,128)(2,1)S(1)} %constant_dynamic-update-slice_fusion.refs_1_), channel_id=1, source_target_pairs={{0,12},{1,13},{2,14},{3,15},{4,0},{5,1},{6,2},{7,3},{8,4},{9,5},{1... | collective-permute-start | bytes 1474568 | tf_op jit(solution)/shard_map/ppermute | solution.py:444
  69.9 5.5 %collective-permute-start.9 = (bf16[8,2,64,128]{3,2,1,0:T(8,128)(2,1)S(1)}, bf16[8,2,64,128]{3,2,1,0:T(8,128)(2,1)S(1)}, u32[]{:S(2)}, u32[]{:S(2)}) collective-permute-start(bf16[8,2,64,128]{3,2,1,0:T(8,128)(2,1)S(1)} %collective-permute-done.8.refs_7_), channel_id=1, source_target_pairs={{0,16},{16,32},{32,48},{48,64},{64,80},{80,96},{96,112},{112,0},{1... | collective-permute-start | bytes 786440 | tf_op jit(solution)/shard_map/ppermute | solution.py:460
  71.2 11.0 %collective-permute-start.5 = (bf16[8,2,64,128]{3,2,1,0:T(8,128)(2,1)S(1)}, bf16[8,2,64,128]{3,2,1,0:T(8,128)(2,1)S(1)}, u32[]{:S(2)}, u32[]{:S(2)}) collective-permute-start(bf16[8,2,64,128]{3,2,1,0:T(8,128)(2,1)S(1)} %collective-permute-done.4.refs_2_), channel_id=1, source_target_pairs={{0,16},{16,32},{32,48},{48,64},{64,80},{80,96},{96,112},{112,0},{1... | collective-permute-start | bytes 786440 | tf_op jit(solution)/shard_map/ppermute | solution.py:460
  75.4 9.5 %collective-permute-start.10 = (bf16[8,2,64,128]{3,2,1,0:T(8,128)(2,1)S(1)}, bf16[8,2,64,128]{3,2,1,0:T(8,128)(2,1)S(1)}, u32[]{:S(2)}, u32[]{:S(2)}) collective-permute-start(bf16[8,2,64,128]{3,2,1,0:T(8,128)(2,1)S(1)} %collective-permute-done.9.refs_8_), channel_id=1, source_target_pairs={{128,240},{144,128},{160,144},{176,160},{192,176},{208,192},{224,2... | collective-permute-start | bytes 786440 | tf_op jit(solution)/shard_map/ppermute | solution.py:460
  79.6 9.3 %collective-permute-start.21 = (bf16[160,1536]{1,0:T(8,128)(2,1)S(1)}, bf16[160,1536]{1,0:T(8,128)(2,1)S(1)}, u32[]{:S(2)}, u32[]{:S(2)}) collective-permute-start(bf16[160,1536]{1,0:T(8,128)(2,1)S(1)} %pad_maximum_fusion.refs_0_), channel_id=1, source_target_pairs={{0,12},{1,13},{2,14},{3,15},{4,0},{5,1},{6,2},{7,3},{8,4},{9,5},{1... | collective-permute-start | bytes 1474568 | tf_op jit(solution)/shard_map/ppermute | solution.py:444
  82.2 9.2 %collective-permute-start.20 = (bf16[160,1536]{1,0:T(8,128)(2,1)S(1)}, bf16[160,1536]{1,0:T(8,128)(2,1)S(1)}, u32[]{:S(2)}, u32[]{:S(2)}) collective-permute-start(bf16[160,1536]{1,0:T(8,128)(2,1)S(1)} %constant_dynamic-update-slice_fusion.refs_1_), channel_id=1, source_target_pairs={{0,4},{1,5},{2,6},{3,7},{4,8},{5,9},{6,10},{7,11},{8,12},{9,13},{1... | collective-permute-start | bytes 1474568 | tf_op jit(solution)/shard_map/ppermute | solution.py:444
  82.2 14.1 %collective-permute-start.23 = (bf16[160,1536]{1,0:T(8,128)(2,1)S(1)}, bf16[160,1536]{1,0:T(8,128)(2,1)S(1)}, u32[]{:S(2)}, u32[]{:S(2)}) collective-permute-start(bf16[160,1536]{1,0:T(8,128)(2,1)S(1)} %collective-permute-done.19.refs_2_), channel_id=1, source_target_pairs={{0,4},{1,5},{2,6},{3,7},{4,8},{5,9},{6,10},{7,11},{8,12},{9,13},{1... | collective-permute-start | bytes 1474568 | tf_op jit(solution)/shard_map/ppermute | solution.py:444
  82.3 14.1 %collective-permute-start.24 = (bf16[160,1536]{1,0:T(8,128)(2,1)S(1)}, bf16[160,1536]{1,0:T(8,128)(2,1)S(1)}, u32[]{:S(2)}, u32[]{:S(2)}) collective-permute-start(bf16[160,1536]{1,0:T(8,128)(2,1)S(1)} %collective-permute-done.22.refs_5_), channel_id=1, source_target_pairs={{0,12},{1,13},{2,14},{3,15},{4,0},{5,1},{6,2},{7,3},{8,4},{9,5},{1... | collective-permute-start | bytes 1474568 | tf_op jit(solution)/shard_map/ppermute | solution.py:444
  84.9 0.7 collective-permute-start.6
  103.3 5.6 %collective-permute-start.25 = (bf16[1536,768]{1,0:T(8,128)(2,1)S(1)}, bf16[1536,768]{1,0:T(8,128)(2,1)S(1)}, u32[]{:S(2)}, u32[]{:S(2)}) collective-permute-start(bf16[1536,768]{1,0:T(8,128)(2,1)S(1)} %get-tuple-element.22), channel_id=1, source_target_pairs={{0,128},{128,0},{1,129},{129,1},{2,130},{130,2},{3,131},{131,3},{4... | collective-permute-start | bytes 7077896 | tf_op jit(solution)/shard_map/ppermute | solution.py:464
where the time goes:
time: 112 us
  starting transfers between devices  54 us (48%)
  Pallas kernels  29.2 us (26%)
  waiting for transfers between devices  19.3 us (17%)
  local copies, waits for them, and re-layouts  5.52 us (5%)
  other arithmetic  2.68 us (2%)
    ppermute x12, starting transfers between devices, along(): return lax.ppermute(array, ALL, pairs)  23.4 us
    ppermute x10, waiting for transfers between devices, turned(): return lax.ppermute(array, PLANE, pairs)  17.7 us
    ppermute x10, starting transfers between devices, turned(): return lax.ppermute(array, PLANE, pairs)  13 us
    pallas_call x1, Pallas kernels, density_call(): pl.pallas_call(density_kernel, out_shape=[jax.ShapeDtypeStruct((N1, 2, BL...  12.7 us
    all_to_all x1, starting transfers between devices, exchange(): col = lax.all_to_all(col, ('gcol_0', 'gcol_1'), 0, 0, tiled=True)  12.5 us
    pallas_call x1, Pallas kernels, away_call(): pl.pallas_call(away_kernel, out_shape=(jax.ShapeDtypeStruct((ROW, NP), BF...  6.93 us
    unnamed x8, local copies, waits for them, and re-layouts  5.46 us
    ppermute x4, starting transfers between devices, swap(): return lax.ppermute(array, 'band', [(0, 1), (1, 0)])  5.15 us
  transfers between devices with their start and end apart: 27, of which 6 were waited for; matrix products, arithmetic and copies ran while one was open for 0% of the time, Pallas kernels for 9%

commit v1 on v0

--- a/solution.py
+++ b/solution.py
@@ -28,7 +28,7 @@
 ROWBLOCK = 120
 COLROWS = GCOL * BLOCK + 4
 WIDTH = NP // LANES
-STEP = 1536
+STEP = 512
 F32, BF16 = jnp.float32, jnp.bfloat16
 VMEM = pltpu.VMEM
 SMEM = pltpu.SMEM
@@ -372,7 +372,7 @@
     )(place, *cols)
 
 
-PIECES = 8
+PIECES = 5
 
 
 def away_kernel(weighted, *refs):
@@ -497,16 +497,14 @@
                 along(ring[-1], lambda f, b, i=i, part=part: 1 if i < 4 or b == part else None)
             )
         rings += ring
-    half = row.shape[0] // 2
+    far = turned(row, 0, 2)
     below, above = turned(row, 0, 1), turned(row, 0, -1)
-    far_a, far_b = turned(below[:half], 0, 1), turned(above[half:], 0, -1)
-    first = jnp.concatenate([row, below], 0)
-    second = jnp.concatenate([above, far_a, far_b], 0)
-    below_a, above_a = turned(first, 1, 1), turned(first, 1, -1)
-    above_b, below_b = turned(second, 1, -1), turned(second, 1, 1)
-    far_a, far_b = turned(below_a, 1, 1), turned(above_b, 1, -1)
+    line = jnp.concatenate([row, below, above, far], 0)
+    half = line.shape[0] // 2
+    below, above = turned(line, 1, 1), turned(line, 1, -1)
+    far_a, far_b = turned(below[:half], 1, 1), turned(above[half:], 1, -1)
     weighted_away, weighted_home = assemble_call(place, rings)
-    pieces = [first, second, below_a, below_b, above_a, above_b, far_a, far_b]
+    pieces = [line, below, above, far_a, far_b]
     away, turned_rows = away_call(weighted_away, pieces)
     received = swap(away)
     home = home_call(weighted_home, turned_rows)

time: 112 us -> 116 us (1.036)
  waiting for transfers between devices: 19.3 us -> 23.9 us
  Pallas kernels: 29.2 us -> 27 us
  starting transfers between devices: 54 us -> 55.5 us
    ppermute x10 -> x7, waiting for transfers between devices: 17.7 us -> 0.43 us  [turned(): return lax.ppermute(array, PLANE, pairs)]
    ppermute x12, waiting for transfers between devices: 1.44 us -> 17.4 us  [along(): return lax.ppermute(array, ALL, pairs)]
    ppermute x4, starting transfers between devices: 5.15 us -> 19.8 us  [swap(): return lax.ppermute(array, 'band', [(0, 1), (1, 0)])]
    all_to_all x1, starting transfers between devices: 12.5 us -> 5.06 us  [exchange(): col = lax.all_to_all(col, ('gcol_0', 'gcol_1'), 0, 0, tiled=True)]
    all_to_all x1, waiting for transfers between devices: 0.01 us -> 6.03 us  [exchange(): col = lax.all_to_all(col, ('gcol_0', 'gcol_1'), 0, 0, tiled=True)]
    ppermute x12, starting transfers between devices: 23.4 us -> 17.8 us  [along(): return lax.ppermute(array, ALL, pairs)]
    pallas_call x1, Pallas kernels: 12.7 us -> 11.5 us  [density_call(): pl.pallas_call(density_kernel, out_shape=[jax.ShapeDtypeStruct((N1, 2, BL...]
    ppermute x10 -> x7, starting transfers between devices: 13 us -> 12.8 us  [turned(): return lax.ppermute(array, PLANE, pairs)]
  transfers between devices with their start and end apart: 27 -> 24, of which waited for: 6 -> 10; matrix products, arithmetic and copies ran while one was open for 0% -> 0% of each run, Pallas kernels for 9% -> 8%
where the time goes in v1:
time: 116 us; the launch traced here: 115 us
  starting transfers between devices  55.5 us (48%)
  Pallas kernels  27 us (23%)
  waiting for transfers between devices  23.9 us (21%)
  local copies, waits for them, and re-layouts  5.53 us (5%)
  other arithmetic  2.71 us (2%)
    ppermute x4, starting transfers between devices, swap(): return lax.ppermute(array, 'band', [(0, 1), (1, 0)])  19.8 us
    ppermute x12, starting transfers between devices, along(): return lax.ppermute(array, ALL, pairs)  17.8 us
    ppermute x12, waiting for transfers between devices, along(): return lax.ppermute(array, ALL, pairs)  17.4 us
    ppermute x7, starting transfers between devices, turned(): return lax.ppermute(array, PLANE, pairs)  12.8 us
    pallas_call x1, Pallas kernels, density_call(): pl.pallas_call(density_kernel, out_shape=[jax.ShapeDtypeStruct((N1, 2, BL...  11.5 us
    all_to_all x1, waiting for transfers between devices, exchange(): col = lax.all_to_all(col, ('gcol_0', 'gcol_1'), 0, 0, tiled=True)  6.03 us
    pallas_call x1, Pallas kernels, away_call(): pl.pallas_call(away_kernel, out_shape=(jax.ShapeDtypeStruct((ROW, NP), BF...  5.94 us
    unnamed x6, local copies, waits for them, and re-layouts  5.43 us
  transfers between devices with their start and end apart: 24, of which 10 were waited for; matrix products, arithmetic and copies ran while one was open for 0% of the time, Pallas kernels for 8%

profile of v1, /device:TPU:1, one launch (start us, length us, event | category | flops | bytes accessed | tf_op | source)
XLA Modules:
  0.0 115.5 jit_solution(4468106716401540887)
XLA Ops:
  0.0 3.2 %collective-permute-start.2 = (bf16[4,98304]{1,0:T(4,128)(2,1)}, bf16[4,98304]{1,0:T(4,128)(2,1)S(1)}, u32[]{:S(2)}, u32[]{:S(2)}) collective-permute-start(bf16[4,98304]{1,0:T(4,128)(2,1)} %refs_0_.1), channel_id=1, source_target_pairs={{0,128},{128,0},{1,129},{129,1},{2,130},{130,2},{3,131},{131,3},{4... | collective-permute-start | bytes 2359304 | tf_op jit(solution)/shard_map/ppermute | solution.py:464
  3.2 0.0 collective-permute-start.1
  3.2 0.5 collective-permute-start
  4.4 0.0 copy-start.2
  4.4 2.1 %ready.1.vals = f32[12352,128]{1,0:T(8,128)S(1)} custom-call(bf16[16,98304]{1,0:T(8,128)(2,1)} %source.1), custom_call_target="tpu_custom_call" | custom-call | tf_op jit(solution)/shard_map/ready/pallas_call | solution.py:83
  6.5 0.0 copy-start
  6.5 2.6 %copy-done = f32[12352,128]{1,0:T(8,128)} copy-done((f32[12352,128]{1,0:T(8,128)}, f32[12352,128]{1,0:T(8,128)S(1)}, u32[]{:S(2)}) %copy-start) | copy-done | bytes 6324248
  9.2 0.0 collective-permute-done.1.other_count
  9.2 0.0 collective-permute-done.other
  9.2 0.0 collective-permute-done.2.refs_1_
  9.2 0.0 copy-done.2
  9.2 0.0 copy-start.1
  9.2 2.8 %copy-done.1 = f32[12352,128]{1,0:T(8,128)S(1)} copy-done((f32[12352,128]{1,0:T(8,128)S(1)}, f32[12352,128]{1,0:T(8,128)}, u32[]{:S(2)}) %copy-start.1) | copy-done | bytes 6324248
  12.0 11.5 %density.1 = (bf16[16,2,64,128]{3,2,1,0:T(8,128)(2,1)}, bf16[2,120,128]{2,1,0:T(8,128)(2,1)S(1)}, bf16[2,120,128]{2,1,0:T(8,128)(2,1)S(1)}, bf16[2,120,128]{2,1,0:T(8,128)(2,1)S(1)}, bf16[2,120,128]{2,1,0:T(8,128)(2,1)S(1)}) custom-call(s32[1]{0:T(128)} %bitcast.place, s32[2,20]{1,0:T(2,128)S(1)} %copy-done.2, s32[2,20]{1,0:T(2,128)S(1)} %collective-permute-done.other, ...), custom_call_target="tpu_custom_call" | custom-call | tf_op jit(solution)/shard_map/density/pallas_call | solution.py:228
  23.5 0.7 collective-permute-start.11
  24.2 4.0 %collective-permute-start.12 = (bf16[2,120,128]{2,1,0:T(8,128)(2,1)S(1)}, bf16[2,120,128]{2,1,0:T(8,128)(2,1)S(1)}, u32[]{:S(2)}, u32[]{:S(2)}) collective-permute-start(bf16[2,120,128]{2,1,0:T(8,128)(2,1)S(1)} %get-tuple-element.18), channel_id=1, source_target_pairs={{0,32},{16,48},{32,64},{48,80},{64,96},{80,112},{96,0},{112,16},{1... | collective-permute-start | bytes 184328 | tf_op jit(solution)/shard_map/ppermute | solution.py:460
  28.2 1.2 %collective-permute-start.13 = (bf16[2,120,128]{2,1,0:T(8,128)(2,1)S(1)}, bf16[2,120,128]{2,1,0:T(8,128)(2,1)S(1)}, u32[]{:S(2)}, u32[]{:S(2)}) collective-permute-start(bf16[2,120,128]{2,1,0:T(8,128)(2,1)S(1)} %get-tuple-element.19), channel_id=1, source_target_pairs={{0,48},{16,64},{32,80},{48,96},{64,112},{80,0},{96,16},{112,32},{1... | collective-permute-start | bytes 184328 | tf_op jit(solution)/shard_map/ppermute | solution.py:460
  29.3 0.4 collective-permute-start.14
  29.8 0.0 collective-permute-done.11.refs_0_
  29.8 0.0 collective-permute-done.12.refs_1_
  29.8 2.4 %collective-permute-done.13.refs_2_ = bf16[2,120,128]{2,1,0:T(8,128)(2,1)S(1)} collective-permute-done((bf16[2,120,128]{2,1,0:T(8,128)(2,1)S(1)}, bf16[2,120,128]{2,1,0:T(8,128)(2,1)S(1)}, u32[]{:S(2)}, u32[]{:S(2)}) %collective-permute-start.13) | collective-permute-done | bytes 61472 | tf_op jit(solution)/shard_map/ppermute | solution.py:460
  32.2 2.1 %collective-permute-done.14.refs_3_ = bf16[2,120,128]{2,1,0:T(8,128)(2,1)S(1)} collective-permute-done((bf16[2,120,128]{2,1,0:T(8,128)(2,1)S(1)}, bf16[2,120,128]{2,1,0:T(8,128)(2,1)S(1)}, u32[]{:S(2)}, u32[]{:S(2)}) %collective-permute-start.14) | collective-permute-done | bytes 61472 | tf_op jit(solution)/shard_map/ppermute | solution.py:460
  34.3 0.1 pack.1
  34.4 7.1 %collective-permute-start.17 = (bf16[80,1536]{1,0:T(8,128)(2,1)S(1)}, bf16[80,1536]{1,0:T(8,128)(2,1)S(1)}, u32[]{:S(2)}, u32[]{:S(2)}) collective-permute-start(bf16[80,1536]{1,0:T(8,128)(2,1)S(1)} %pack.1), channel_id=1, source_target_pairs={{0,2},{1,3},{2,0},{3,1},{4,6},{5,7},{6,4},{7,5},{8,10},{9,11},{10,... | collective-permute-start | bytes 737288 | tf_op jit(solution)/shard_map/ppermute | solution.py:444
  41.5 0.0 collective-permute-start.16
  41.5 1.5 %collective-permute-start.15 = (bf16[80,1536]{1,0:T(8,128)(2,1)S(1)}, bf16[80,1536]{1,0:T(8,128)(2,1)S(1)}, u32[]{:S(2)}, u32[]{:S(2)}) collective-permute-start(bf16[80,1536]{1,0:T(8,128)(2,1)S(1)} %pack.1), channel_id=1, source_target_pairs={{0,1},{1,2},{2,3},{3,0},{4,5},{5,6},{6,7},{7,4},{8,9},{9,10},{10,1... | collective-permute-start | bytes 737288 | tf_op jit(solution)/shard_map/ppermute | solution.py:444
  43.0 5.1 %all-to-all-start = ((bf16[16,2,64,128]{3,2,1,0:T(8,128)(2,1)}), bf16[16,2,64,128]{3,2,1,0:T(8,128)(2,1)S(1)}, u32[]{:S(2)}, u32[]{:S(2)}) async-start(bf16[16,2,64,128]{3,2,1,0:T(8,128)(2,1)} %get-tuple-element.14), calls=%async_computation | async-start | bytes 1048576 | tf_op jit(solution)/shard_map/all_to_all | solution.py:489
  48.1 0.0 collective-permute-done.17
  48.1 0.4 collective-permute-done.16
  48.5 0.0 collective-permute-done.15
  48.5 0.1 pad_maximum_fusion.refs_0_
  48.6 2.6 %collective-permute-start.19 = (bf16[320,1536]{1,0:T(8,128)(2,1)S(1)}, bf16[320,1536]{1,0:T(8,128)(2,1)S(1)}, u32[]{:S(2)}, u32[]{:S(2)}) collective-permute-start(bf16[320,1536]{1,0:T(8,128)(2,1)S(1)} %pad_maximum_fusion.refs_0_), channel_id=1, source_target_pairs={{0,12},{1,13},{2,14},{3,15},{4,0},{5,1},{6,2},{7,3},{8,4},{9,5},{1... | collective-permute-start | bytes 2949128 | tf_op jit(solution)/shard_map/ppermute | solution.py:444
  51.1 0.0 collective-permute-start.18
  51.1 6.0 %all-to-all-done = bf16[16,2,64,128]{3,2,1,0:T(8,128)(2,1)S(1)} async-done(((bf16[16,2,64,128]{3,2,1,0:T(8,128)(2,1)}), bf16[16,2,64,128]{3,2,1,0:T(8,128)(2,1)S(1)}, u32[]{:S(2)}, u32[]{:S(2)}) %all-to-all-start) | async-done | bytes 524320 | tf_op jit(solution)/shard_map/all_to_all | solution.py:489
  57.2 0.5 collective-permute-start.7
  57.7 1.2 %collective-permute-start.3 = (bf16[8,2,64,128]{3,2,1,0:T(8,128)(2,1)S(1)}, bf16[8,2,64,128]{3,2,1,0:T(8,128)(2,1)S(1)}, u32[]{:S(2)}, u32[]{:S(2)}) collective-permute-start(bf16[8,2,64,128]{3,2,1,0:T(8,128)(2,1)S(1)} %get-tuple-element.24.refs_0_), channel_id=1, source_target_pairs={{0,16},{16,32},{32,48},{48,64},{64,80},{80,96},{96,112},{112,0},{1... | collective-permute-start | bytes 786440 | tf_op jit(solution)/shard_map/ppermute | solution.py:460
  58.9 4.1 %collective-permute-done.7.refs_6_ = bf16[8,2,64,128]{3,2,1,0:T(8,128)(2,1)S(1)} collective-permute-done((bf16[8,2,64,128]{3,2,1,0:T(8,128)(2,1)S(1)}, bf16[8,2,64,128]{3,2,1,0:T(8,128)(2,1)S(1)}, u32[]{:S(2)}, u32[]{:S(2)}) %collective-permute-start.7) | collective-permute-done | bytes 262176 | tf_op jit(solution)/shard_map/ppermute | solution.py:460
  63.0 1.5 %collective-permute-start.8 = (bf16[8,2,64,128]{3,2,1,0:T(8,128)(2,1)S(1)}, bf16[8,2,64,128]{3,2,1,0:T(8,128)(2,1)S(1)}, u32[]{:S(2)}, u32[]{:S(2)}) collective-permute-start(bf16[8,2,64,128]{3,2,1,0:T(8,128)(2,1)S(1)} %collective-permute-done.7.refs_6_), channel_id=1, source_target_pairs={{0,16},{16,32},{32,48},{48,64},{64,80},{80,96},{96,112},{112,0},{1... | collective-permute-start | bytes 786440 | tf_op jit(solution)/shard_map/ppermute | solution.py:460
  64.4 1.3 %collective-permute-done.3.refs_1_ = bf16[8,2,64,128]{3,2,1,0:T(8,128)(2,1)S(1)} collective-permute-done((bf16[8,2,64,128]{3,2,1,0:T(8,128)(2,1)S(1)}, bf16[8,2,64,128]{3,2,1,0:T(8,128)(2,1)S(1)}, u32[]{:S(2)}, u32[]{:S(2)}) %collective-permute-start.3) | collective-permute-done | bytes 262176 | tf_op jit(solution)/shard_map/ppermute | solution.py:460
  65.8 1.5 %collective-permute-start.4 = (bf16[8,2,64,128]{3,2,1,0:T(8,128)(2,1)S(1)}, bf16[8,2,64,128]{3,2,1,0:T(8,128)(2,1)S(1)}, u32[]{:S(2)}, u32[]{:S(2)}) collective-permute-start(bf16[8,2,64,128]{3,2,1,0:T(8,128)(2,1)S(1)} %collective-permute-done.3.refs_1_), channel_id=1, source_target_pairs={{0,16},{16,32},{32,48},{48,64},{64,80},{80,96},{96,112},{112,0},{1... | collective-permute-start | bytes 786440 | tf_op jit(solution)/shard_map/ppermute | solution.py:460
  67.2 2.7 %collective-permute-done.8.refs_7_ = bf16[8,2,64,128]{3,2,1,0:T(8,128)(2,1)S(1)} collective-permute-done((bf16[8,2,64,128]{3,2,1,0:T(8,128)(2,1)S(1)}, bf16[8,2,64,128]{3,2,1,0:T(8,128)(2,1)S(1)}, u32[]{:S(2)}, u32[]{:S(2)}) %collective-permute-start.8) | collective-permute-done | bytes 262176 | tf_op jit(solution)/shard_map/ppermute | solution.py:460
  70.0 1.2 %collective-permute-start.9 = (bf16[8,2,64,128]{3,2,1,0:T(8,128)(2,1)S(1)}, bf16[8,2,64,128]{3,2,1,0:T(8,128)(2,1)S(1)}, u32[]{:S(2)}, u32[]{:S(2)}) collective-permute-start(bf16[8,2,64,128]{3,2,1,0:T(8,128)(2,1)S(1)} %collective-permute-done.8.refs_7_), channel_id=1, source_target_pairs={{0,16},{16,32},{32,48},{48,64},{64,80},{80,96},{96,112},{112,0},{1... | collective-permute-start | bytes 786440 | tf_op jit(solution)/shard_map/ppermute | solution.py:460
  71.2 1.6 %collective-permute-done.4.refs_2_ = bf16[8,2,64,128]{3,2,1,0:T(8,128)(2,1)S(1)} collective-permute-done((bf16[8,2,64,128]{3,2,1,0:T(8,128)(2,1)S(1)}, bf16[8,2,64,128]{3,2,1,0:T(8,128)(2,1)S(1)}, u32[]{:S(2)}, u32[]{:S(2)}) %collective-permute-start.4) | collective-permute-done | bytes 262176 | tf_op jit(solution)/shard_map/ppermute | solution.py:460
  72.8 1.2 %collective-permute-start.5 = (bf16[8,2,64,128]{3,2,1,0:T(8,128)(2,1)S(1)}, bf16[8,2,64,128]{3,2,1,0:T(8,128)(2,1)S(1)}, u32[]{:S(2)}, u32[]{:S(2)}) collective-permute-start(bf16[8,2,64,128]{3,2,1,0:T(8,128)(2,1)S(1)} %collective-permute-done.4.refs_2_), channel_id=1, source_target_pairs={{0,16},{16,32},{32,48},{48,64},{64,80},{80,96},{96,112},{112,0},{1... | collective-permute-start | bytes 786440 | tf_op jit(solution)/shard_map/ppermute | solution.py:460
  74.0 0.0 collective-permute-done.19.refs_2_
  74.0 1.0 collective-permute-start.21
  75.0 0.0 collective-permute-done.18.refs_1_
  75.0 0.6 collective-permute-start.20
  75.7 0.0 collective-permute-done.9.refs_8_
  75.7 3.8 %collective-permute-start.10 = (bf16[8,2,64,128]{3,2,1,0:T(8,128)(2,1)S(1)}, bf16[8,2,64,128]{3,2,1,0:T(8,128)(2,1)S(1)}, u32[]{:S(2)}, u32[]{:S(2)}) collective-permute-start(bf16[8,2,64,128]{3,2,1,0:T(8,128)(2,1)S(1)} %collective-permute-done.9.refs_8_), channel_id=1, source_target_pairs={{128,240},{144,128},{160,144},{176,160},{192,176},{208,192},{224,2... | collective-permute-start | bytes 786440 | tf_op jit(solution)/shard_map/ppermute | solution.py:460
  79.5 0.0 collective-permute-done.5.refs_3_
  79.5 0.7 collective-permute-start.6
  80.2 3.1 %collective-permute-done.10.refs_9_ = bf16[8,2,64,128]{3,2,1,0:T(8,128)(2,1)S(1)} collective-permute-done((bf16[8,2,64,128]{3,2,1,0:T(8,128)(2,1)S(1)}, bf16[8,2,64,128]{3,2,1,0:T(8,128)(2,1)S(1)}, u32[]{:S(2)}, u32[]{:S(2)}) %collective-permute-start.10) | collective-permute-done | bytes 262176 | tf_op jit(solution)/shard_map/ppermute | solution.py:460
  83.3 0.0 collective-permute-done.6.refs_4_
  83.3 3.2 %assemble.1 = (bf16[1280,768]{1,0:T(8,128)(2,1)S(1)}, bf16[1280,768]{1,0:T(8,128)(2,1)S(1)}) custom-call(s32[1]{0:T(128)} %bitcast.place, bf16[8,2,64,128]{3,2,1,0:T(8,128)(2,1)S(1)} %get-tuple-element.24.refs_0_, bf16[8,2,64,128]{3,2,1,0:T(8,128)(2,1)S(1)} %collective-permute-done.3.refs_1_, bf16[8,2,64,128]{3,2,1,0:T(8,128)(2,1)S(1)} %collective-permute-done.4.refs_2_, ...), custom_call_target="tpu_custom_call" | custom-call | tf_op jit(solution)/shard_map/assemble/pallas_call | solution.py:363
  86.6 0.0 collective-permute-done.21.refs_4_
  86.6 0.0 collective-permute-done.20.refs_3_
  86.6 5.9 %away.1 = (bf16[1536,768]{1,0:T(8,128)(2,1)S(1)}, bf16[1536,1280]{1,0:T(8,128)(2,1)S(1)}) custom-call(bf16[1280,768]{1,0:T(8,128)(2,1)S(1)} %get-tuple-element.16.weighted, bf16[320,1536]{1,0:T(8,128)(2,1)S(1)} %pad_maximum_fusion.refs_0_, bf16[320,1536]{1,0:T(8,128)(2,1)S(1)} %collective-permute-done.18.refs_1_, ...), custom_call_target="tpu_custom_call" | custom-call | tf_op jit(solution)/shard_map/away/pallas_call | solution.py:396
  92.5 16.1 %collective-permute-start.22 = (bf16[1536,768]{1,0:T(8,128)(2,1)S(1)}, bf16[1536,768]{1,0:T(8,128)(2,1)S(1)}, u32[]{:S(2)}, u32[]{:S(2)}) collective-permute-start(bf16[1536,768]{1,0:T(8,128)(2,1)S(1)} %get-tuple-element.22), channel_id=1, source_target_pairs={{0,128},{128,0},{1,129},{129,1},{2,130},{130,2},{3,131},{131,3},{4... | collective-permute-start | bytes 7077896 | tf_op jit(solution)/shard_map/ppermute | solution.py:464
  108.7 4.1 %home.1 = f32[1536,768]{1,0:T(8,128)S(1)} custom-call(bf16[1280,768]{1,0:T(8,128)(2,1)S(1)} %get-tuple-element.15.weighted, bf16[1536,1280]{1,0:T(8,128)(2,1)S(1)} %get-tuple-element.21.rows), custom_call_target="tpu_custom_call" | custom-call | tf_op jit(solution)/shard_map/home/pallas_call | solution.py:422
  112.7 0.1 collective-permute-done.22
  112.8 2.6 %negate_bitcast_fusion = f32[1,1536,768]{2,1,0:T(8,128)} fusion(f32[1536,768]{1,0:T(8,128)S(1)} %home.1, bf16[1536,768]{1,0:T(8,128)(2,1)S(1)} %collective-permute-done.22), kind=kLoop, calls=%fused_computation | loop fusion | flops 3538944 | bytes 11796480 | tf_op jit(solution)/shard_map/neg | solution.py:511
  (3 shorter events, 0.1 us)
Async XLA Ops:
  0.0 9.2 %collective-permute-start.2 = (bf16[4,98304]{1,0:T(4,128)(2,1)}, bf16[4,98304]{1,0:T(4,128)(2,1)S(1)}, u32[]{:S(2)}, u32[]{:S(2)}) collective-permute-start(bf16[4,98304]{1,0:T(4,128)(2,1)} %refs_0_.1), channel_id=1, source_target_pairs={{0,128},{128,0},{1,129},{129,1},{2,130},{130,2},{3,131},{131,3},{4... | collective-permute-start | bytes 2359304 | tf_op jit(solution)/shard_map/ppermute | solution.py:464
  3.2 6.0 %collective-permute-start.1 = (s32[1]{0:T(128)}, s32[1]{0:T(128)}, u32[]{:S(2)}, u32[]{:S(2)}) collective-permute-start(s32[1]{0:T(128)} %param.17), channel_id=1, source_target_pairs={{0,128},{128,0},{1,129},{129,1},{2,130},{130,2},{3,131},{131,3},{4... | collective-permute-start | bytes 20 | tf_op jit(solution)/shard_map/ppermute | solution.py:464
  3.2 6.0 %collective-permute-start = (s32[2,20]{1,0:T(2,128)}, s32[2,20]{1,0:T(2,128)S(1)}, u32[]{:S(2)}, u32[]{:S(2)}) collective-permute-start(s32[2,20]{1,0:T(2,128)} %mine.1), channel_id=1, source_target_pairs={{0,128},{128,0},{1,129},{129,1},{2,130},{130,2},{3,131},{131,3},{4... | collective-permute-start | bytes 488 | tf_op jit(solution)/shard_map/ppermute | solution.py:464
  4.4 4.8 %copy-start.2 = (s32[2,20]{1,0:T(2,128)S(1)}, s32[2,20]{1,0:T(2,128)}, u32[]{:S(2)}) copy-start(s32[2,20]{1,0:T(2,128)} %mine.1) | copy-start | bytes 484
  6.5 2.6 %copy-start = (f32[12352,128]{1,0:T(8,128)}, f32[12352,128]{1,0:T(8,128)S(1)}, u32[]{:S(2)}) copy-start(f32[12352,128]{1,0:T(8,128)S(1)} %ready.1.vals) | copy-start | bytes 18972676
  9.2 2.8 %copy-start.1 = (f32[12352,128]{1,0:T(8,128)S(1)}, f32[12352,128]{1,0:T(8,128)}, u32[]{:S(2)}) copy-start(f32[12352,128]{1,0:T(8,128)} %copy-done) | copy-start | bytes 18972676
  23.5 6.2 %collective-permute-start.11 = (bf16[2,120,128]{2,1,0:T(8,128)(2,1)S(1)}, bf16[2,120,128]{2,1,0:T(8,128)(2,1)S(1)}, u32[]{:S(2)}, u32[]{:S(2)}) collective-permute-start(bf16[2,120,128]{2,1,0:T(8,128)(2,1)S(1)} %get-tuple-element.17), channel_id=1, source_target_pairs={{0,16},{16,32},{32,48},{48,64},{64,80},{80,96},{96,112},{112,0},{1... | collective-permute-start | bytes 184328 | tf_op jit(solution)/shard_map/ppermute | solution.py:460
  24.2 5.6 %collective-permute-start.12 = (bf16[2,120,128]{2,1,0:T(8,128)(2,1)S(1)}, bf16[2,120,128]{2,1,0:T(8,128)(2,1)S(1)}, u32[]{:S(2)}, u32[]{:S(2)}) collective-permute-start(bf16[2,120,128]{2,1,0:T(8,128)(2,1)S(1)} %get-tuple-element.18), channel_id=1, source_target_pairs={{0,32},{16,48},{32,64},{48,80},{64,96},{80,112},{96,0},{112,16},{1... | collective-permute-start | bytes 184328 | tf_op jit(solution)/shard_map/ppermute | solution.py:460
  28.2 4.1 %collective-permute-start.13 = (bf16[2,120,128]{2,1,0:T(8,128)(2,1)S(1)}, bf16[2,120,128]{2,1,0:T(8,128)(2,1)S(1)}, u32[]{:S(2)}, u32[]{:S(2)}) collective-permute-start(bf16[2,120,128]{2,1,0:T(8,128)(2,1)S(1)} %get-tuple-element.19), channel_id=1, source_target_pairs={{0,48},{16,64},{32,80},{48,96},{64,112},{80,0},{96,16},{112,32},{1... | collective-permute-start | bytes 184328 | tf_op jit(solution)/shard_map/ppermute | solution.py:460
  29.3 5.0 %collective-permute-start.14 = (bf16[2,120,128]{2,1,0:T(8,128)(2,1)S(1)}, bf16[2,120,128]{2,1,0:T(8,128)(2,1)S(1)}, u32[]{:S(2)}, u32[]{:S(2)}) collective-permute-start(bf16[2,120,128]{2,1,0:T(8,128)(2,1)S(1)} %get-tuple-element.20), channel_id=1, source_target_pairs={{0,64},{16,80},{32,96},{48,112},{64,0},{80,16},{96,32},{112,48},{1... | collective-permute-start | bytes 184328 | tf_op jit(solution)/shard_map/ppermute | solution.py:460
  34.4 13.7 %collective-permute-start.17 = (bf16[80,1536]{1,0:T(8,128)(2,1)S(1)}, bf16[80,1536]{1,0:T(8,128)(2,1)S(1)}, u32[]{:S(2)}, u32[]{:S(2)}) collective-permute-start(bf16[80,1536]{1,0:T(8,128)(2,1)S(1)} %pack.1), channel_id=1, source_target_pairs={{0,2},{1,3},{2,0},{3,1},{4,6},{5,7},{6,4},{7,5},{8,10},{9,11},{10,... | collective-permute-start | bytes 737288 | tf_op jit(solution)/shard_map/ppermute | solution.py:444
  41.5 7.0 %collective-permute-start.16 = (bf16[80,1536]{1,0:T(8,128)(2,1)S(1)}, bf16[80,1536]{1,0:T(8,128)(2,1)S(1)}, u32[]{:S(2)}, u32[]{:S(2)}) collective-permute-start(bf16[80,1536]{1,0:T(8,128)(2,1)S(1)} %pack.1), channel_id=1, source_target_pairs={{0,3},{1,0},{2,1},{3,2},{4,7},{5,4},{6,5},{7,6},{8,11},{9,8},{10,9... | collective-permute-start | bytes 737288 | tf_op jit(solution)/shard_map/ppermute | solution.py:444
  41.5 7.0 %collective-permute-start.15 = (bf16[80,1536]{1,0:T(8,128)(2,1)S(1)}, bf16[80,1536]{1,0:T(8,128)(2,1)S(1)}, u32[]{:S(2)}, u32[]{:S(2)}) collective-permute-start(bf16[80,1536]{1,0:T(8,128)(2,1)S(1)} %pack.1), channel_id=1, source_target_pairs={{0,1},{1,2},{2,3},{3,0},{4,5},{5,6},{6,7},{7,4},{8,9},{9,10},{10,1... | collective-permute-start | bytes 737288 | tf_op jit(solution)/shard_map/ppermute | solution.py:444
  43.0 14.2 %all-to-all-start = ((bf16[16,2,64,128]{3,2,1,0:T(8,128)(2,1)}), bf16[16,2,64,128]{3,2,1,0:T(8,128)(2,1)S(1)}, u32[]{:S(2)}, u32[]{:S(2)}) async-start(bf16[16,2,64,128]{3,2,1,0:T(8,128)(2,1)} %get-tuple-element.14), calls=%async_computation | async-start | bytes 1048576 | tf_op jit(solution)/shard_map/all_to_all | solution.py:489
  48.6 25.4 %collective-permute-start.19 = (bf16[320,1536]{1,0:T(8,128)(2,1)S(1)}, bf16[320,1536]{1,0:T(8,128)(2,1)S(1)}, u32[]{:S(2)}, u32[]{:S(2)}) collective-permute-start(bf16[320,1536]{1,0:T(8,128)(2,1)S(1)} %pad_maximum_fusion.refs_0_), channel_id=1, source_target_pairs={{0,12},{1,13},{2,14},{3,15},{4,0},{5,1},{6,2},{7,3},{8,4},{9,5},{1... | collective-permute-start | bytes 2949128 | tf_op jit(solution)/shard_map/ppermute | solution.py:444
  51.1 23.9 %collective-permute-start.18 = (bf16[320,1536]{1,0:T(8,128)(2,1)S(1)}, bf16[320,1536]{1,0:T(8,128)(2,1)S(1)}, u32[]{:S(2)}, u32[]{:S(2)}) collective-permute-start(bf16[320,1536]{1,0:T(8,128)(2,1)S(1)} %pad_maximum_fusion.refs_0_), channel_id=1, source_target_pairs={{0,4},{1,5},{2,6},{3,7},{4,8},{5,9},{6,10},{7,11},{8,12},{9,13},{1... | collective-permute-start | bytes 2949128 | tf_op jit(solution)/shard_map/ppermute | solution.py:444
  57.2 5.8 %collective-permute-start.7 = (bf16[8,2,64,128]{3,2,1,0:T(8,128)(2,1)S(1)}, bf16[8,2,64,128]{3,2,1,0:T(8,128)(2,1)S(1)}, u32[]{:S(2)}, u32[]{:S(2)}) collective-permute-start(bf16[8,2,64,128]{3,2,1,0:T(8,128)(2,1)S(1)} %get-tuple-element.23.refs_5_), channel_id=1, source_target_pairs={{0,16},{16,32},{32,48},{48,64},{64,80},{80,96},{96,112},{112,0},{1... | collective-permute-start | bytes 786440 | tf_op jit(solution)/shard_map/ppermute | solution.py:460
  57.7 8.1 %collective-permute-start.3 = (bf16[8,2,64,128]{3,2,1,0:T(8,128)(2,1)S(1)}, bf16[8,2,64,128]{3,2,1,0:T(8,128)(2,1)S(1)}, u32[]{:S(2)}, u32[]{:S(2)}) collective-permute-start(bf16[8,2,64,128]{3,2,1,0:T(8,128)(2,1)S(1)} %get-tuple-element.24.refs_0_), channel_id=1, source_target_pairs={{0,16},{16,32},{32,48},{48,64},{64,80},{80,96},{96,112},{112,0},{1... | collective-permute-start | bytes 786440 | tf_op jit(solution)/shard_map/ppermute | solution.py:460
  63.0 7.0 %collective-permute-start.8 = (bf16[8,2,64,128]{3,2,1,0:T(8,128)(2,1)S(1)}, bf16[8,2,64,128]{3,2,1,0:T(8,128)(2,1)S(1)}, u32[]{:S(2)}, u32[]{:S(2)}) collective-permute-start(bf16[8,2,64,128]{3,2,1,0:T(8,128)(2,1)S(1)} %collective-permute-done.7.refs_6_), channel_id=1, source_target_pairs={{0,16},{16,32},{32,48},{48,64},{64,80},{80,96},{96,112},{112,0},{1... | collective-permute-start | bytes 786440 | tf_op jit(solution)/shard_map/ppermute | solution.py:460
  65.8 7.0 %collective-permute-start.4 = (bf16[8,2,64,128]{3,2,1,0:T(8,128)(2,1)S(1)}, bf16[8,2,64,128]{3,2,1,0:T(8,128)(2,1)S(1)}, u32[]{:S(2)}, u32[]{:S(2)}) collective-permute-start(bf16[8,2,64,128]{3,2,1,0:T(8,128)(2,1)S(1)} %collective-permute-done.3.refs_1_), channel_id=1, source_target_pairs={{0,16},{16,32},{32,48},{48,64},{64,80},{80,96},{96,112},{112,0},{1... | collective-permute-start | bytes 786440 | tf_op jit(solution)/shard_map/ppermute | solution.py:460
  70.0 5.7 %collective-permute-start.9 = (bf16[8,2,64,128]{3,2,1,0:T(8,128)(2,1)S(1)}, bf16[8,2,64,128]{3,2,1,0:T(8,128)(2,1)S(1)}, u32[]{:S(2)}, u32[]{:S(2)}) collective-permute-start(bf16[8,2,64,128]{3,2,1,0:T(8,128)(2,1)S(1)} %collective-permute-done.8.refs_7_), channel_id=1, source_target_pairs={{0,16},{16,32},{32,48},{48,64},{64,80},{80,96},{96,112},{112,0},{1... | collective-permute-start | bytes 786440 | tf_op jit(solution)/shard_map/ppermute | solution.py:460
  72.8 6.7 %collective-permute-start.5 = (bf16[8,2,64,128]{3,2,1,0:T(8,128)(2,1)S(1)}, bf16[8,2,64,128]{3,2,1,0:T(8,128)(2,1)S(1)}, u32[]{:S(2)}, u32[]{:S(2)}) collective-permute-start(bf16[8,2,64,128]{3,2,1,0:T(8,128)(2,1)S(1)} %collective-permute-done.4.refs_2_), channel_id=1, source_target_pairs={{0,16},{16,32},{32,48},{48,64},{64,80},{80,96},{96,112},{112,0},{1... | collective-permute-start | bytes 786440 | tf_op jit(solution)/shard_map/ppermute | solution.py:460
  74.0 12.5 %collective-permute-start.21 = (bf16[160,1536]{1,0:T(8,128)(2,1)S(1)}, bf16[160,1536]{1,0:T(8,128)(2,1)S(1)}, u32[]{:S(2)}, u32[]{:S(2)}) collective-permute-start(bf16[160,1536]{1,0:T(8,128)(2,1)S(1)} %slice.19), channel_id=1, source_target_pairs={{0,12},{1,13},{2,14},{3,15},{4,0},{5,1},{6,2},{7,3},{8,4},{9,5},{1... | collective-permute-start | bytes 1474568 | tf_op jit(solution)/shard_map/ppermute | solution.py:444
  75.0 11.5 %collective-permute-start.20 = (bf16[160,1536]{1,0:T(8,128)(2,1)S(1)}, bf16[160,1536]{1,0:T(8,128)(2,1)S(1)}, u32[]{:S(2)}, u32[]{:S(2)}) collective-permute-start(bf16[160,1536]{1,0:T(8,128)(2,1)S(1)} %slice.18), channel_id=1, source_target_pairs={{0,4},{1,5},{2,6},{3,7},{4,8},{5,9},{6,10},{7,11},{8,12},{9,13},{1... | collective-permute-start | bytes 1474568 | tf_op jit(solution)/shard_map/ppermute | solution.py:444
  75.7 7.7 %collective-permute-start.10 = (bf16[8,2,64,128]{3,2,1,0:T(8,128)(2,1)S(1)}, bf16[8,2,64,128]{3,2,1,0:T(8,128)(2,1)S(1)}, u32[]{:S(2)}, u32[]{:S(2)}) collective-permute-start(bf16[8,2,64,128]{3,2,1,0:T(8,128)(2,1)S(1)} %collective-permute-done.9.refs_8_), channel_id=1, source_target_pairs={{128,240},{144,128},{160,144},{176,160},{192,176},{208,192},{224,2... | collective-permute-start | bytes 786440 | tf_op jit(solution)/shard_map/ppermute | solution.py:460
  79.5 3.8 %collective-permute-start.6 = (bf16[8,2,64,128]{3,2,1,0:T(8,128)(2,1)S(1)}, bf16[8,2,64,128]{3,2,1,0:T(8,128)(2,1)S(1)}, u32[]{:S(2)}, u32[]{:S(2)}) collective-permute-start(bf16[8,2,64,128]{3,2,1,0:T(8,128)(2,1)S(1)} %collective-permute-done.5.refs_3_), channel_id=1, source_target_pairs={{0,16},{16,32},{32,48},{48,64},{64,80},{80,96},{96,112},{112,0},{1... | collective-permute-start | bytes 786440 | tf_op jit(solution)/shard_map/ppermute | solution.py:460
  92.5 20.3 %collective-permute-start.22 = (bf16[1536,768]{1,0:T(8,128)(2,1)S(1)}, bf16[1536,768]{1,0:T(8,128)(2,1)S(1)}, u32[]{:S(2)}, u32[]{:S(2)}) collective-permute-start(bf16[1536,768]{1,0:T(8,128)(2,1)S(1)} %get-tuple-element.22), channel_id=1, source_target_pairs={{0,128},{128,0},{1,129},{129,1},{2,130},{130,2},{3,131},{131,3},{4... | collective-permute-start | bytes 7077896 | tf_op jit(solution)/shard_map/ppermute | solution.py:464

commit v2 on v1

--- a/solution.py
+++ b/solution.py
@@ -253,7 +253,7 @@
             SMEM((1024,), F32),
             pltpu.SemaphoreType.DMA((9,)),
         ],
-        compiler_params=pltpu.CompilerParams(vmem_limit_bytes=26 << 20),
+        compiler_params=pltpu.CompilerParams(vmem_limit_bytes=24 << 20),
         interpret=interpret,
         name="density",
     )(place, mine, other, my_count, other_count, vals, stay(con_mine), con_other, stay(second), stay(third),
@@ -302,9 +302,32 @@
     return jnp.where(step == 0, 0, jnp.where(step == 1, 3, jnp.where(step == 2, 1, 2)))
 
 
+def choose_kernel(place, one, two, out):
+    @pl.when(place[0] < GROW * GCOL)
+    def _():
+        out[...] = one[...]
+
+    @pl.when(place[0] >= GROW * GCOL)
+    def _():
+        out[...] = two[...]
+
+
+def choose_call(place, one, two, interpret=False):
+    vmem = pl.BlockSpec(memory_space=VMEM)
+    return pl.pallas_call(
+        choose_kernel,
+        out_shape=jax.ShapeDtypeStruct(one.shape, one.dtype),
+        in_specs=[pl.BlockSpec(memory_space=SMEM), vmem, vmem],
+        out_specs=vmem,
+        compiler_params=pltpu.CompilerParams(vmem_limit_bytes=4 << 20),
+        interpret=interpret,
+        name="choose",
+    )(place, one, two)
+
+
 def assemble_kernel(place, *refs):
-    cols = refs[:10]
-    away_out, home_out, spread = refs[10:]
+    cols = [*refs[:4], refs[8], *refs[4:9]]
+    away_out, home_out, spread = refs[9:]
     me = place[0]
     band, y, x = me >> 7, (me >> 2) & 3, me & 3
 
@@ -363,7 +386,7 @@
     return pl.pallas_call(
         assemble_kernel,
         out_shape=[jax.ShapeDtypeStruct((PANEL, NP), BF16)] * 2,
-        in_specs=[pl.BlockSpec(memory_space=SMEM)] + [vmem] * 10,
+        in_specs=[pl.BlockSpec(memory_space=SMEM)] + [vmem] * 9,
         out_specs=[vmem] * 2,
         scratch_shapes=[VMEM((GROW * COLROWS, LANES), F32)],
         compiler_params=pltpu.CompilerParams(vmem_limit_bytes=14 << 20),
@@ -489,14 +512,12 @@
     col = lax.all_to_all(col, ("gcol_0", "gcol_1"), 0, 0, tiled=True)
     row = pack_call(rows)
     parts = [col[:8], col[8:]]
-    rings = []
-    for part in range(2):
-        ring = [parts[part]]
-        for i in range(1, 5):
-            ring.append(
-                along(ring[-1], lambda f, b, i=i, part=part: 1 if i < 4 or b == part else None)
-            )
-        rings += ring
+    rings = [[part] for part in parts]
+    for _ in range(1, 4):
+        for part in range(2):
+            rings[part].append(along(rings[part][-1], lambda f, b: 1))
+    last = choose_call(place, rings[0][-1], rings[1][-1])
+    rings = rings[0] + rings[1] + [along(last, lambda f, b: 1)]
     far = turned(row, 0, 2)
     below, above = turned(row, 0, 1), turned(row, 0, -1)
     line = jnp.concatenate([row, below, above, far], 0)

time: 116 us -> 114 us (0.983)
  starting transfers between devices: 55.5 us -> 50 us
  waiting for transfers between devices: 23.9 us -> 27.6 us
    ppermute x12 -> x11, waiting for transfers between devices: 17.4 us -> 21.1 us  [along(): return lax.ppermute(array, ALL, pairs)]
    ppermute x4, starting transfers between devices: 19.8 us -> 16.8 us  [swap(): return lax.ppermute(array, 'band', [(0, 1), (1, 0)])]
    ppermute x12 -> x11, starting transfers between devices: 17.8 us -> 15.4 us  [along(): return lax.ppermute(array, ALL, pairs)]
  transfers between devices with their start and end apart: 24 -> 23, of which waited for: 10 -> 11; matrix products, arithmetic and copies ran while one was open for 0% -> 0% of each run, Pallas kernels for 8% -> 8%
where the time goes in v2:
time: 114 us
  starting transfers between devices  50 us (44%)
  waiting for transfers between devices  27.6 us (24%)
  Pallas kernels  26.9 us (24%)
  local copies, waits for them, and re-layouts  5.52 us (5%)
  other arithmetic  2.71 us (2%)
    ppermute x11, waiting for transfers between devices, along(): return lax.ppermute(array, ALL, pairs)  21.1 us
    ppermute x4, starting transfers between devices, swap(): return lax.ppermute(array, 'band', [(0, 1), (1, 0)])  16.8 us
    ppermute x11, starting transfers between devices, along(): return lax.ppermute(array, ALL, pairs)  15.4 us
    ppermute x7, starting transfers between devices, turned(): return lax.ppermute(array, PLANE, pairs)  12.8 us
    pallas_call x1, Pallas kernels, density_call(): pl.pallas_call(density_kernel, out_shape=[jax.ShapeDtypeStruct((N1, 2, BL...  11.5 us
    all_to_all x1, waiting for transfers between devices, exchange(): col = lax.all_to_all(col, ('gcol_0', 'gcol_1'), 0, 0, tiled=True)  6.03 us
    pallas_call x1, Pallas kernels, away_call(): pl.pallas_call(away_kernel, out_shape=(jax.ShapeDtypeStruct((ROW, NP), BF...  5.95 us
    unnamed x6, local copies, waits for them, and re-layouts  5.42 us
  transfers between devices with their start and end apart: 23, of which 11 were waited for; matrix products, arithmetic and copies ran while one was open for 0% of the time, Pallas kernels for 8%

profile of v2, /device:TPU:1, one launch (start us, length us, event | category | flops | bytes accessed | tf_op | source)
XLA Modules:
  0.0 113.6 jit_solution(6869053503324758605)
XLA Ops:
  0.0 3.2 %collective-permute-start.2 = (bf16[4,98304]{1,0:T(4,128)(2,1)}, bf16[4,98304]{1,0:T(4,128)(2,1)S(1)}, u32[]{:S(2)}, u32[]{:S(2)}) collective-permute-start(bf16[4,98304]{1,0:T(4,128)(2,1)} %refs_0_.1), channel_id=1, source_target_pairs={{0,128},{128,0},{1,129},{129,1},{2,130},{130,2},{3,131},{131,3},{4... | collective-permute-start | bytes 2359304 | tf_op jit(solution)/shard_map/ppermute | solution.py:487
  3.2 0.0 collective-permute-start.1
  3.2 0.5 collective-permute-start
  4.4 0.0 copy-start.2
  4.4 2.1 %ready.1.vals = f32[12352,128]{1,0:T(8,128)S(1)} custom-call(bf16[16,98304]{1,0:T(8,128)(2,1)} %source.1), custom_call_target="tpu_custom_call" | custom-call | tf_op jit(solution)/shard_map/ready/pallas_call | solution.py:83
  6.5 0.0 copy-start
  6.5 2.6 %copy-done = f32[12352,128]{1,0:T(8,128)} copy-done((f32[12352,128]{1,0:T(8,128)}, f32[12352,128]{1,0:T(8,128)S(1)}, u32[]{:S(2)}) %copy-start) | copy-done | bytes 6324248
  9.2 0.0 collective-permute-done.1.other_count
  9.2 0.0 collective-permute-done.other
  9.2 0.0 collective-permute-done.2.refs_1_
  9.2 0.0 copy-done.2
  9.2 0.0 copy-start.1
  9.2 2.8 %copy-done.1 = f32[12352,128]{1,0:T(8,128)S(1)} copy-done((f32[12352,128]{1,0:T(8,128)S(1)}, f32[12352,128]{1,0:T(8,128)}, u32[]{:S(2)}) %copy-start.1) | copy-done | bytes 6324248
  12.0 11.5 %density.1 = (bf16[16,2,64,128]{3,2,1,0:T(8,128)(2,1)}, bf16[2,120,128]{2,1,0:T(8,128)(2,1)S(1)}, bf16[2,120,128]{2,1,0:T(8,128)(2,1)S(1)}, bf16[2,120,128]{2,1,0:T(8,128)(2,1)S(1)}, bf16[2,120,128]{2,1,0:T(8,128)(2,1)S(1)}) custom-call(s32[1]{0:T(128)} %bitcast.place, s32[2,20]{1,0:T(2,128)S(1)} %copy-done.2, s32[2,20]{1,0:T(2,128)S(1)} %collective-permute-done.other, ...), custom_call_target="tpu_custom_call" | custom-call | tf_op jit(solution)/shard_map/density/pallas_call | solution.py:228
  23.5 0.7 collective-permute-start.10
  24.1 4.0 %collective-permute-start.11 = (bf16[2,120,128]{2,1,0:T(8,128)(2,1)S(1)}, bf16[2,120,128]{2,1,0:T(8,128)(2,1)S(1)}, u32[]{:S(2)}, u32[]{:S(2)}) collective-permute-start(bf16[2,120,128]{2,1,0:T(8,128)(2,1)S(1)} %get-tuple-element.18), channel_id=1, source_target_pairs={{0,32},{16,48},{32,64},{48,80},{64,96},{80,112},{96,0},{112,16},{1... | collective-permute-start | bytes 184328 | tf_op jit(solution)/shard_map/ppermute | solution.py:483
  28.1 1.2 %collective-permute-start.12 = (bf16[2,120,128]{2,1,0:T(8,128)(2,1)S(1)}, bf16[2,120,128]{2,1,0:T(8,128)(2,1)S(1)}, u32[]{:S(2)}, u32[]{:S(2)}) collective-permute-start(bf16[2,120,128]{2,1,0:T(8,128)(2,1)S(1)} %get-tuple-element.19), channel_id=1, source_target_pairs={{0,48},{16,64},{32,80},{48,96},{64,112},{80,0},{96,16},{112,32},{1... | collective-permute-start | bytes 184328 | tf_op jit(solution)/shard_map/ppermute | solution.py:483
  29.3 0.4 collective-permute-start.13
  29.7 0.0 collective-permute-done.10.refs_0_
  29.7 0.0 collective-permute-done.11.refs_1_
  29.7 2.4 %collective-permute-done.12.refs_2_ = bf16[2,120,128]{2,1,0:T(8,128)(2,1)S(1)} collective-permute-done((bf16[2,120,128]{2,1,0:T(8,128)(2,1)S(1)}, bf16[2,120,128]{2,1,0:T(8,128)(2,1)S(1)}, u32[]{:S(2)}, u32[]{:S(2)}) %collective-permute-start.12) | collective-permute-done | bytes 61472 | tf_op jit(solution)/shard_map/ppermute | solution.py:483
  32.2 2.1 %collective-permute-done.13.refs_3_ = bf16[2,120,128]{2,1,0:T(8,128)(2,1)S(1)} collective-permute-done((bf16[2,120,128]{2,1,0:T(8,128)(2,1)S(1)}, bf16[2,120,128]{2,1,0:T(8,128)(2,1)S(1)}, u32[]{:S(2)}, u32[]{:S(2)}) %collective-permute-start.13) | collective-permute-done | bytes 61472 | tf_op jit(solution)/shard_map/ppermute | solution.py:483
  34.2 0.1 pack.1
  34.3 7.1 %collective-permute-start.16 = (bf16[80,1536]{1,0:T(8,128)(2,1)S(1)}, bf16[80,1536]{1,0:T(8,128)(2,1)S(1)}, u32[]{:S(2)}, u32[]{:S(2)}) collective-permute-start(bf16[80,1536]{1,0:T(8,128)(2,1)S(1)} %pack.1), channel_id=1, source_target_pairs={{0,2},{1,3},{2,0},{3,1},{4,6},{5,7},{6,4},{7,5},{8,10},{9,11},{10,... | collective-permute-start | bytes 737288 | tf_op jit(solution)/shard_map/ppermute | solution.py:467
  41.5 0.0 collective-permute-start.15
  41.5 1.5 %collective-permute-start.14 = (bf16[80,1536]{1,0:T(8,128)(2,1)S(1)}, bf16[80,1536]{1,0:T(8,128)(2,1)S(1)}, u32[]{:S(2)}, u32[]{:S(2)}) collective-permute-start(bf16[80,1536]{1,0:T(8,128)(2,1)S(1)} %pack.1), channel_id=1, source_target_pairs={{0,1},{1,2},{2,3},{3,0},{4,5},{5,6},{6,7},{7,4},{8,9},{9,10},{10,1... | collective-permute-start | bytes 737288 | tf_op jit(solution)/shard_map/ppermute | solution.py:467
  42.9 5.0 %all-to-all-start = ((bf16[16,2,64,128]{3,2,1,0:T(8,128)(2,1)}), bf16[16,2,64,128]{3,2,1,0:T(8,128)(2,1)S(1)}, u32[]{:S(2)}, u32[]{:S(2)}) async-start(bf16[16,2,64,128]{3,2,1,0:T(8,128)(2,1)} %get-tuple-element.14), calls=%async_computation | async-start | bytes 1048576 | tf_op jit(solution)/shard_map/all_to_all | solution.py:512
  48.0 0.0 collective-permute-done.16
  48.0 0.4 collective-permute-done.15
  48.4 0.0 collective-permute-done.14
  48.4 0.1 pad_maximum_fusion.refs_0_
  48.5 2.6 %collective-permute-start.18 = (bf16[320,1536]{1,0:T(8,128)(2,1)S(1)}, bf16[320,1536]{1,0:T(8,128)(2,1)S(1)}, u32[]{:S(2)}, u32[]{:S(2)}) collective-permute-start(bf16[320,1536]{1,0:T(8,128)(2,1)S(1)} %pad_maximum_fusion.refs_0_), channel_id=1, source_target_pairs={{0,12},{1,13},{2,14},{3,15},{4,0},{5,1},{6,2},{7,3},{8,4},{9,5},{1... | collective-permute-start | bytes 2949128 | tf_op jit(solution)/shard_map/ppermute | solution.py:467
  51.0 0.0 collective-permute-start.17
  51.0 6.0 %all-to-all-done = bf16[16,2,64,128]{3,2,1,0:T(8,128)(2,1)S(1)} async-done(((bf16[16,2,64,128]{3,2,1,0:T(8,128)(2,1)}), bf16[16,2,64,128]{3,2,1,0:T(8,128)(2,1)S(1)}, u32[]{:S(2)}, u32[]{:S(2)}) %all-to-all-start) | async-done | bytes 524320 | tf_op jit(solution)/shard_map/all_to_all | solution.py:512
  57.1 0.5 collective-permute-start.6
  57.6 1.2 %collective-permute-start.3 = (bf16[8,2,64,128]{3,2,1,0:T(8,128)(2,1)S(1)}, bf16[8,2,64,128]{3,2,1,0:T(8,128)(2,1)S(1)}, u32[]{:S(2)}, u32[]{:S(2)}) collective-permute-start(bf16[8,2,64,128]{3,2,1,0:T(8,128)(2,1)S(1)} %get-tuple-element.24.refs_0_), channel_id=1, source_target_pairs={{0,16},{16,32},{32,48},{48,64},{64,80},{80,96},{96,112},{112,0},{1... | collective-permute-start | bytes 786440 | tf_op jit(solution)/shard_map/ppermute | solution.py:483
  58.8 4.1 %collective-permute-done.6.refs_5_ = bf16[8,2,64,128]{3,2,1,0:T(8,128)(2,1)S(1)} collective-permute-done((bf16[8,2,64,128]{3,2,1,0:T(8,128)(2,1)S(1)}, bf16[8,2,64,128]{3,2,1,0:T(8,128)(2,1)S(1)}, u32[]{:S(2)}, u32[]{:S(2)}) %collective-permute-start.6) | collective-permute-done | bytes 262176 | tf_op jit(solution)/shard_map/ppermute | solution.py:483
  62.9 1.5 %collective-permute-start.7 = (bf16[8,2,64,128]{3,2,1,0:T(8,128)(2,1)S(1)}, bf16[8,2,64,128]{3,2,1,0:T(8,128)(2,1)S(1)}, u32[]{:S(2)}, u32[]{:S(2)}) collective-permute-start(bf16[8,2,64,128]{3,2,1,0:T(8,128)(2,1)S(1)} %collective-permute-done.6.refs_5_), channel_id=1, source_target_pairs={{0,16},{16,32},{32,48},{48,64},{64,80},{80,96},{96,112},{112,0},{1... | collective-permute-start | bytes 786440 | tf_op jit(solution)/shard_map/ppermute | solution.py:483
  64.4 1.3 %collective-permute-done.3.refs_1_ = bf16[8,2,64,128]{3,2,1,0:T(8,128)(2,1)S(1)} collective-permute-done((bf16[8,2,64,128]{3,2,1,0:T(8,128)(2,1)S(1)}, bf16[8,2,64,128]{3,2,1,0:T(8,128)(2,1)S(1)}, u32[]{:S(2)}, u32[]{:S(2)}) %collective-permute-start.3) | collective-permute-done | bytes 262176 | tf_op jit(solution)/shard_map/ppermute | solution.py:483
  65.7 1.5 %collective-permute-start.4 = (bf16[8,2,64,128]{3,2,1,0:T(8,128)(2,1)S(1)}, bf16[8,2,64,128]{3,2,1,0:T(8,128)(2,1)S(1)}, u32[]{:S(2)}, u32[]{:S(2)}) collective-permute-start(bf16[8,2,64,128]{3,2,1,0:T(8,128)(2,1)S(1)} %collective-permute-done.3.refs_1_), channel_id=1, source_target_pairs={{0,16},{16,32},{32,48},{48,64},{64,80},{80,96},{96,112},{112,0},{1... | collective-permute-start | bytes 786440 | tf_op jit(solution)/shard_map/ppermute | solution.py:483
  67.2 2.7 %collective-permute-done.7.refs_6_ = bf16[8,2,64,128]{3,2,1,0:T(8,128)(2,1)S(1)} collective-permute-done((bf16[8,2,64,128]{3,2,1,0:T(8,128)(2,1)S(1)}, bf16[8,2,64,128]{3,2,1,0:T(8,128)(2,1)S(1)}, u32[]{:S(2)}, u32[]{:S(2)}) %collective-permute-start.7) | collective-permute-done | bytes 262176 | tf_op jit(solution)/shard_map/ppermute | solution.py:483
  69.9 1.2 %collective-permute-start.8 = (bf16[8,2,64,128]{3,2,1,0:T(8,128)(2,1)S(1)}, bf16[8,2,64,128]{3,2,1,0:T(8,128)(2,1)S(1)}, u32[]{:S(2)}, u32[]{:S(2)}) collective-permute-start(bf16[8,2,64,128]{3,2,1,0:T(8,128)(2,1)S(1)} %collective-permute-done.7.refs_6_), channel_id=1, source_target_pairs={{0,16},{16,32},{32,48},{48,64},{64,80},{80,96},{96,112},{112,0},{1... | collective-permute-start | bytes 786440 | tf_op jit(solution)/shard_map/ppermute | solution.py:483
  71.1 1.6 %collective-permute-done.4.refs_2_ = bf16[8,2,64,128]{3,2,1,0:T(8,128)(2,1)S(1)} collective-permute-done((bf16[8,2,64,128]{3,2,1,0:T(8,128)(2,1)S(1)}, bf16[8,2,64,128]{3,2,1,0:T(8,128)(2,1)S(1)}, u32[]{:S(2)}, u32[]{:S(2)}) %collective-permute-start.4) | collective-permute-done | bytes 262176 | tf_op jit(solution)/shard_map/ppermute | solution.py:483
  72.7 1.2 %collective-permute-start.5 = (bf16[8,2,64,128]{3,2,1,0:T(8,128)(2,1)S(1)}, bf16[8,2,64,128]{3,2,1,0:T(8,128)(2,1)S(1)}, u32[]{:S(2)}, u32[]{:S(2)}) collective-permute-start(bf16[8,2,64,128]{3,2,1,0:T(8,128)(2,1)S(1)} %collective-permute-done.4.refs_2_), channel_id=1, source_target_pairs={{0,16},{16,32},{32,48},{48,64},{64,80},{80,96},{96,112},{112,0},{1... | collective-permute-start | bytes 786440 | tf_op jit(solution)/shard_map/ppermute | solution.py:483
  73.9 0.0 collective-permute-done.18.refs_2_
  73.9 1.0 collective-permute-start.20
  74.9 0.0 collective-permute-done.17.refs_1_
  75.0 0.6 collective-permute-start.19
  75.6 0.0 collective-permute-done.8.two.refs_7_
  75.6 2.7 %collective-permute-done.5.one.refs_3_ = bf16[8,2,64,128]{3,2,1,0:T(8,128)(2,1)S(1)} collective-permute-done((bf16[8,2,64,128]{3,2,1,0:T(8,128)(2,1)S(1)}, bf16[8,2,64,128]{3,2,1,0:T(8,128)(2,1)S(1)}, u32[]{:S(2)}, u32[]{:S(2)}) %collective-permute-start.5) | collective-permute-done | bytes 262176 | tf_op jit(solution)/shard_map/ppermute | solution.py:483
  78.3 2.1 %collective-permute-start.9 = (bf16[8,2,64,128]{3,2,1,0:T(8,128)(2,1)S(1)}, bf16[8,2,64,128]{3,2,1,0:T(8,128)(2,1)S(1)}, u32[]{:S(2)}, u32[]{:S(2)}) collective-permute-start(bf16[8,2,64,128]{3,2,1,0:T(8,128)(2,1)S(1)} %choose.1), channel_id=1, source_target_pairs={{0,16},{16,32},{32,48},{48,64},{64,80},{80,96},{96,112},{112,0},{1... | collective-permute-start | bytes 786440 | tf_op jit(solution)/shard_map/ppermute | solution.py:483
  80.4 4.1 %collective-permute-done.9.refs_8_ = bf16[8,2,64,128]{3,2,1,0:T(8,128)(2,1)S(1)} collective-permute-done((bf16[8,2,64,128]{3,2,1,0:T(8,128)(2,1)S(1)}, bf16[8,2,64,128]{3,2,1,0:T(8,128)(2,1)S(1)}, u32[]{:S(2)}, u32[]{:S(2)}) %collective-permute-start.9) | collective-permute-done | bytes 262176 | tf_op jit(solution)/shard_map/ppermute | solution.py:483
  84.5 3.2 %assemble.1 = (bf16[1280,768]{1,0:T(8,128)(2,1)S(1)}, bf16[1280,768]{1,0:T(8,128)(2,1)S(1)}) custom-call(s32[1]{0:T(128)} %bitcast.place, bf16[8,2,64,128]{3,2,1,0:T(8,128)(2,1)S(1)} %get-tuple-element.24.refs_0_, bf16[8,2,64,128]{3,2,1,0:T(8,128)(2,1)S(1)} %collective-permute-done.3.refs_1_, bf16[8,2,64,128]{3,2,1,0:T(8,128)(2,1)S(1)} %collective-permute-done.4.refs_2_, ...), custom_call_target="tpu_custom_call" | custom-call | tf_op jit(solution)/shard_map/assemble/pallas_call | solution.py:386
  87.7 0.0 collective-permute-done.20.refs_4_
  87.8 0.0 collective-permute-done.19.refs_3_
  87.8 5.9 %away.1 = (bf16[1536,768]{1,0:T(8,128)(2,1)S(1)}, bf16[1536,1280]{1,0:T(8,128)(2,1)S(1)}) custom-call(bf16[1280,768]{1,0:T(8,128)(2,1)S(1)} %get-tuple-element.16.weighted, bf16[320,1536]{1,0:T(8,128)(2,1)S(1)} %pad_maximum_fusion.refs_0_, bf16[320,1536]{1,0:T(8,128)(2,1)S(1)} %collective-permute-done.17.refs_1_, ...), custom_call_target="tpu_custom_call" | custom-call | tf_op jit(solution)/shard_map/away/pallas_call | solution.py:419
  93.7 13.1 %collective-permute-start.21 = (bf16[1536,768]{1,0:T(8,128)(2,1)S(1)}, bf16[1536,768]{1,0:T(8,128)(2,1)S(1)}, u32[]{:S(2)}, u32[]{:S(2)}) collective-permute-start(bf16[1536,768]{1,0:T(8,128)(2,1)S(1)} %get-tuple-element.22), channel_id=1, source_target_pairs={{0,128},{128,0},{1,129},{129,1},{2,130},{130,2},{3,131},{131,3},{4... | collective-permute-start | bytes 7077896 | tf_op jit(solution)/shard_map/ppermute | solution.py:487
  106.8 4.1 %home.1 = f32[1536,768]{1,0:T(8,128)S(1)} custom-call(bf16[1280,768]{1,0:T(8,128)(2,1)S(1)} %get-tuple-element.15.weighted, bf16[1536,1280]{1,0:T(8,128)(2,1)S(1)} %get-tuple-element.21.rows), custom_call_target="tpu_custom_call" | custom-call | tf_op jit(solution)/shard_map/home/pallas_call | solution.py:445
  110.9 0.1 collective-permute-done.21
  111.0 2.6 %negate_bitcast_fusion = f32[1,1536,768]{2,1,0:T(8,128)} fusion(f32[1536,768]{1,0:T(8,128)S(1)} %home.1, bf16[1536,768]{1,0:T(8,128)(2,1)S(1)} %collective-permute-done.21), kind=kLoop, calls=%fused_computation | loop fusion | flops 3538944 | bytes 11796480 | tf_op jit(solution)/shard_map/neg | solution.py:532
  (4 shorter events, 0.1 us)
Async XLA Ops:
  0.0 9.2 %collective-permute-start.2 = (bf16[4,98304]{1,0:T(4,128)(2,1)}, bf16[4,98304]{1,0:T(4,128)(2,1)S(1)}, u32[]{:S(2)}, u32[]{:S(2)}) collective-permute-start(bf16[4,98304]{1,0:T(4,128)(2,1)} %refs_0_.1), channel_id=1, source_target_pairs={{0,128},{128,0},{1,129},{129,1},{2,130},{130,2},{3,131},{131,3},{4... | collective-permute-start | bytes 2359304 | tf_op jit(solution)/shard_map/ppermute | solution.py:487
  3.2 6.0 %collective-permute-start.1 = (s32[1]{0:T(128)}, s32[1]{0:T(128)}, u32[]{:S(2)}, u32[]{:S(2)}) collective-permute-start(s32[1]{0:T(128)} %param.17), channel_id=1, source_target_pairs={{0,128},{128,0},{1,129},{129,1},{2,130},{130,2},{3,131},{131,3},{4... | collective-permute-start | bytes 20 | tf_op jit(solution)/shard_map/ppermute | solution.py:487
  3.2 6.0 %collective-permute-start = (s32[2,20]{1,0:T(2,128)}, s32[2,20]{1,0:T(2,128)S(1)}, u32[]{:S(2)}, u32[]{:S(2)}) collective-permute-start(s32[2,20]{1,0:T(2,128)} %mine.1), channel_id=1, source_target_pairs={{0,128},{128,0},{1,129},{129,1},{2,130},{130,2},{3,131},{131,3},{4... | collective-permute-start | bytes 488 | tf_op jit(solution)/shard_map/ppermute | solution.py:487
  4.4 4.8 %copy-start.2 = (s32[2,20]{1,0:T(2,128)S(1)}, s32[2,20]{1,0:T(2,128)}, u32[]{:S(2)}) copy-start(s32[2,20]{1,0:T(2,128)} %mine.1) | copy-start | bytes 484
  6.5 2.6 %copy-start = (f32[12352,128]{1,0:T(8,128)}, f32[12352,128]{1,0:T(8,128)S(1)}, u32[]{:S(2)}) copy-start(f32[12352,128]{1,0:T(8,128)S(1)} %ready.1.vals) | copy-start | bytes 18972676
  9.2 2.8 %copy-start.1 = (f32[12352,128]{1,0:T(8,128)S(1)}, f32[12352,128]{1,0:T(8,128)}, u32[]{:S(2)}) copy-start(f32[12352,128]{1,0:T(8,128)} %copy-done) | copy-start | bytes 18972676
  23.5 6.2 %collective-permute-start.10 = (bf16[2,120,128]{2,1,0:T(8,128)(2,1)S(1)}, bf16[2,120,128]{2,1,0:T(8,128)(2,1)S(1)}, u32[]{:S(2)}, u32[]{:S(2)}) collective-permute-start(bf16[2,120,128]{2,1,0:T(8,128)(2,1)S(1)} %get-tuple-element.17), channel_id=1, source_target_pairs={{0,16},{16,32},{32,48},{48,64},{64,80},{80,96},{96,112},{112,0},{1... | collective-permute-start | bytes 184328 | tf_op jit(solution)/shard_map/ppermute | solution.py:483
  24.1 5.6 %collective-permute-start.11 = (bf16[2,120,128]{2,1,0:T(8,128)(2,1)S(1)}, bf16[2,120,128]{2,1,0:T(8,128)(2,1)S(1)}, u32[]{:S(2)}, u32[]{:S(2)}) collective-permute-start(bf16[2,120,128]{2,1,0:T(8,128)(2,1)S(1)} %get-tuple-element.18), channel_id=1, source_target_pairs={{0,32},{16,48},{32,64},{48,80},{64,96},{80,112},{96,0},{112,16},{1... | collective-permute-start | bytes 184328 | tf_op jit(solution)/shard_map/ppermute | solution.py:483
  28.1 4.1 %collective-permute-start.12 = (bf16[2,120,128]{2,1,0:T(8,128)(2,1)S(1)}, bf16[2,120,128]{2,1,0:T(8,128)(2,1)S(1)}, u32[]{:S(2)}, u32[]{:S(2)}) collective-permute-start(bf16[2,120,128]{2,1,0:T(8,128)(2,1)S(1)} %get-tuple-element.19), channel_id=1, source_target_pairs={{0,48},{16,64},{32,80},{48,96},{64,112},{80,0},{96,16},{112,32},{1... | collective-permute-start | bytes 184328 | tf_op jit(solution)/shard_map/ppermute | solution.py:483
  29.3 5.0 %collective-permute-start.13 = (bf16[2,120,128]{2,1,0:T(8,128)(2,1)S(1)}, bf16[2,120,128]{2,1,0:T(8,128)(2,1)S(1)}, u32[]{:S(2)}, u32[]{:S(2)}) collective-permute-start(bf16[2,120,128]{2,1,0:T(8,128)(2,1)S(1)} %get-tuple-element.20), channel_id=1, source_target_pairs={{0,64},{16,80},{32,96},{48,112},{64,0},{80,16},{96,32},{112,48},{1... | collective-permute-start | bytes 184328 | tf_op jit(solution)/shard_map/ppermute | solution.py:483
  34.3 13.7 %collective-permute-start.16 = (bf16[80,1536]{1,0:T(8,128)(2,1)S(1)}, bf16[80,1536]{1,0:T(8,128)(2,1)S(1)}, u32[]{:S(2)}, u32[]{:S(2)}) collective-permute-start(bf16[80,1536]{1,0:T(8,128)(2,1)S(1)} %pack.1), channel_id=1, source_target_pairs={{0,2},{1,3},{2,0},{3,1},{4,6},{5,7},{6,4},{7,5},{8,10},{9,11},{10,... | collective-permute-start | bytes 737288 | tf_op jit(solution)/shard_map/ppermute | solution.py:467
  41.5 6.9 %collective-permute-start.15 = (bf16[80,1536]{1,0:T(8,128)(2,1)S(1)}, bf16[80,1536]{1,0:T(8,128)(2,1)S(1)}, u32[]{:S(2)}, u32[]{:S(2)}) collective-permute-start(bf16[80,1536]{1,0:T(8,128)(2,1)S(1)} %pack.1), channel_id=1, source_target_pairs={{0,3},{1,0},{2,1},{3,2},{4,7},{5,4},{6,5},{7,6},{8,11},{9,8},{10,9... | collective-permute-start | bytes 737288 | tf_op jit(solution)/shard_map/ppermute | solution.py:467
  41.5 6.9 %collective-permute-start.14 = (bf16[80,1536]{1,0:T(8,128)(2,1)S(1)}, bf16[80,1536]{1,0:T(8,128)(2,1)S(1)}, u32[]{:S(2)}, u32[]{:S(2)}) collective-permute-start(bf16[80,1536]{1,0:T(8,128)(2,1)S(1)} %pack.1), channel_id=1, source_target_pairs={{0,1},{1,2},{2,3},{3,0},{4,5},{5,6},{6,7},{7,4},{8,9},{9,10},{10,1... | collective-permute-start | bytes 737288 | tf_op jit(solution)/shard_map/ppermute | solution.py:467
  42.9 14.1 %all-to-all-start = ((bf16[16,2,64,128]{3,2,1,0:T(8,128)(2,1)}), bf16[16,2,64,128]{3,2,1,0:T(8,128)(2,1)S(1)}, u32[]{:S(2)}, u32[]{:S(2)}) async-start(bf16[16,2,64,128]{3,2,1,0:T(8,128)(2,1)} %get-tuple-element.14), calls=%async_computation | async-start | bytes 1048576 | tf_op jit(solution)/shard_map/all_to_all | solution.py:512
  48.5 25.4 %collective-permute-start.18 = (bf16[320,1536]{1,0:T(8,128)(2,1)S(1)}, bf16[320,1536]{1,0:T(8,128)(2,1)S(1)}, u32[]{:S(2)}, u32[]{:S(2)}) collective-permute-start(bf16[320,1536]{1,0:T(8,128)(2,1)S(1)} %pad_maximum_fusion.refs_0_), channel_id=1, source_target_pairs={{0,12},{1,13},{2,14},{3,15},{4,0},{5,1},{6,2},{7,3},{8,4},{9,5},{1... | collective-permute-start | bytes 2949128 | tf_op jit(solution)/shard_map/ppermute | solution.py:467
  51.0 23.9 %collective-permute-start.17 = (bf16[320,1536]{1,0:T(8,128)(2,1)S(1)}, bf16[320,1536]{1,0:T(8,128)(2,1)S(1)}, u32[]{:S(2)}, u32[]{:S(2)}) collective-permute-start(bf16[320,1536]{1,0:T(8,128)(2,1)S(1)} %pad_maximum_fusion.refs_0_), channel_id=1, source_target_pairs={{0,4},{1,5},{2,6},{3,7},{4,8},{5,9},{6,10},{7,11},{8,12},{9,13},{1... | collective-permute-start | bytes 2949128 | tf_op jit(solution)/shard_map/ppermute | solution.py:467
  57.1 5.8 %collective-permute-start.6 = (bf16[8,2,64,128]{3,2,1,0:T(8,128)(2,1)S(1)}, bf16[8,2,64,128]{3,2,1,0:T(8,128)(2,1)S(1)}, u32[]{:S(2)}, u32[]{:S(2)}) collective-permute-start(bf16[8,2,64,128]{3,2,1,0:T(8,128)(2,1)S(1)} %get-tuple-element.23.refs_4_), channel_id=1, source_target_pairs={{0,16},{16,32},{32,48},{48,64},{64,80},{80,96},{96,112},{112,0},{1... | collective-permute-start | bytes 786440 | tf_op jit(solution)/shard_map/ppermute | solution.py:483
  57.6 8.1 %collective-permute-start.3 = (bf16[8,2,64,128]{3,2,1,0:T(8,128)(2,1)S(1)}, bf16[8,2,64,128]{3,2,1,0:T(8,128)(2,1)S(1)}, u32[]{:S(2)}, u32[]{:S(2)}) collective-permute-start(bf16[8,2,64,128]{3,2,1,0:T(8,128)(2,1)S(1)} %get-tuple-element.24.refs_0_), channel_id=1, source_target_pairs={{0,16},{16,32},{32,48},{48,64},{64,80},{80,96},{96,112},{112,0},{1... | collective-permute-start | bytes 786440 | tf_op jit(solution)/shard_map/ppermute | solution.py:483
  62.9 7.0 %collective-permute-start.7 = (bf16[8,2,64,128]{3,2,1,0:T(8,128)(2,1)S(1)}, bf16[8,2,64,128]{3,2,1,0:T(8,128)(2,1)S(1)}, u32[]{:S(2)}, u32[]{:S(2)}) collective-permute-start(bf16[8,2,64,128]{3,2,1,0:T(8,128)(2,1)S(1)} %collective-permute-done.6.refs_5_), channel_id=1, source_target_pairs={{0,16},{16,32},{32,48},{48,64},{64,80},{80,96},{96,112},{112,0},{1... | collective-permute-start | bytes 786440 | tf_op jit(solution)/shard_map/ppermute | solution.py:483
  65.7 7.0 %collective-permute-start.4 = (bf16[8,2,64,128]{3,2,1,0:T(8,128)(2,1)S(1)}, bf16[8,2,64,128]{3,2,1,0:T(8,128)(2,1)S(1)}, u32[]{:S(2)}, u32[]{:S(2)}) collective-permute-start(bf16[8,2,64,128]{3,2,1,0:T(8,128)(2,1)S(1)} %collective-permute-done.3.refs_1_), channel_id=1, source_target_pairs={{0,16},{16,32},{32,48},{48,64},{64,80},{80,96},{96,112},{112,0},{1... | collective-permute-start | bytes 786440 | tf_op jit(solution)/shard_map/ppermute | solution.py:483
  69.9 5.7 %collective-permute-start.8 = (bf16[8,2,64,128]{3,2,1,0:T(8,128)(2,1)S(1)}, bf16[8,2,64,128]{3,2,1,0:T(8,128)(2,1)S(1)}, u32[]{:S(2)}, u32[]{:S(2)}) collective-permute-start(bf16[8,2,64,128]{3,2,1,0:T(8,128)(2,1)S(1)} %collective-permute-done.7.refs_6_), channel_id=1, source_target_pairs={{0,16},{16,32},{32,48},{48,64},{64,80},{80,96},{96,112},{112,0},{1... | collective-permute-start | bytes 786440 | tf_op jit(solution)/shard_map/ppermute | solution.py:483
  72.7 5.6 %collective-permute-start.5 = (bf16[8,2,64,128]{3,2,1,0:T(8,128)(2,1)S(1)}, bf16[8,2,64,128]{3,2,1,0:T(8,128)(2,1)S(1)}, u32[]{:S(2)}, u32[]{:S(2)}) collective-permute-start(bf16[8,2,64,128]{3,2,1,0:T(8,128)(2,1)S(1)} %collective-permute-done.4.refs_2_), channel_id=1, source_target_pairs={{0,16},{16,32},{32,48},{48,64},{64,80},{80,96},{96,112},{112,0},{1... | collective-permute-start | bytes 786440 | tf_op jit(solution)/shard_map/ppermute | solution.py:483
  73.9 13.8 %collective-permute-start.20 = (bf16[160,1536]{1,0:T(8,128)(2,1)S(1)}, bf16[160,1536]{1,0:T(8,128)(2,1)S(1)}, u32[]{:S(2)}, u32[]{:S(2)}) collective-permute-start(bf16[160,1536]{1,0:T(8,128)(2,1)S(1)} %slice.19), channel_id=1, source_target_pairs={{0,12},{1,13},{2,14},{3,15},{4,0},{5,1},{6,2},{7,3},{8,4},{9,5},{1... | collective-permute-start | bytes 1474568 | tf_op jit(solution)/shard_map/ppermute | solution.py:467
  75.0 12.8 %collective-permute-start.19 = (bf16[160,1536]{1,0:T(8,128)(2,1)S(1)}, bf16[160,1536]{1,0:T(8,128)(2,1)S(1)}, u32[]{:S(2)}, u32[]{:S(2)}) collective-permute-start(bf16[160,1536]{1,0:T(8,128)(2,1)S(1)} %slice.18), channel_id=1, source_target_pairs={{0,4},{1,5},{2,6},{3,7},{4,8},{5,9},{6,10},{7,11},{8,12},{9,13},{1... | collective-permute-start | bytes 1474568 | tf_op jit(solution)/shard_map/ppermute | solution.py:467
  78.3 6.2 %collective-permute-start.9 = (bf16[8,2,64,128]{3,2,1,0:T(8,128)(2,1)S(1)}, bf16[8,2,64,128]{3,2,1,0:T(8,128)(2,1)S(1)}, u32[]{:S(2)}, u32[]{:S(2)}) collective-permute-start(bf16[8,2,64,128]{3,2,1,0:T(8,128)(2,1)S(1)} %choose.1), channel_id=1, source_target_pairs={{0,16},{16,32},{32,48},{48,64},{64,80},{80,96},{96,112},{112,0},{1... | collective-permute-start | bytes 786440 | tf_op jit(solution)/shard_map/ppermute | solution.py:483
  93.7 17.3 %collective-permute-start.21 = (bf16[1536,768]{1,0:T(8,128)(2,1)S(1)}, bf16[1536,768]{1,0:T(8,128)(2,1)S(1)}, u32[]{:S(2)}, u32[]{:S(2)}) collective-permute-start(bf16[1536,768]{1,0:T(8,128)(2,1)S(1)} %get-tuple-element.22), channel_id=1, source_target_pairs={{0,128},{128,0},{1,129},{129,1},{2,130},{130,2},{3,131},{131,3},{4... | collective-permute-start | bytes 7077896 | tf_op jit(solution)/shard_map/ppermute | solution.py:487

commit v3 on v1

--- a/solution.py
+++ b/solution.py
@@ -97,16 +97,15 @@
 ):
     hbm, refs = refs[:9], refs[9:]
     col_out = refs[0]
-    row_outs = refs[1:5]
-    cons, lhs, acc, table_a, table_b, done, lines, row_lines = refs[5:13]
-    local, sems = refs[13:22], refs[22]
+    row_outs = refs[1:6]
+    cons, lhs, acc, table_a, table_b, done, lines, row_lines = refs[6:14]
+    local, sems = refs[14:23], refs[23]
     copies = [pltpu.make_async_copy(a, b, sems.at[i]) for i, (a, b) in enumerate(zip(hbm, local))]
     for copy in copies:
         copy.start()
     con_mine, con_other, second, third, mix_hi, mix_lo, scale, val_e, con_e = local
     band = place[0] >> 7
     z = (place[0] >> 4) & 7
-    skip = jnp.where((band == 0) == ((place[0] & 15) < 8), 1, 0)
     for copy in copies[:2]:
         copy.wait()
 
@@ -197,20 +196,42 @@
         lines[WIDTH * HALF + 1 : WIDTH * HALF + 2, :] = w_mid
         lines[WIDTH * HALF + 2 : WIDTH * HALF + 3, :] = weight - w_hi - w_mid
         lines[WIDTH * HALF + 3 : WIDTH * HALF + 4, :] = jnp.zeros((1, LANES), F32)
-        for k in range(N1):
-            block = done[k * 16 : (k + 1) * 16, :] * (scale[:, k * NP : (k + 1) * NP] * norm)
-            done[k * 16 : (k + 1) * 16, :] = block
-            for ch in range(WIDTH):
-                lines[ch * HALF : (ch + 1) * HALF, :] = block[:HALF, ch * LANES : (ch + 1) * LANES]
-            col_out[k, h] = lines[...].astype(BF16)
-        for i in range(4):
-            target = jnp.where(band == 0, z + i + skip, z - i - skip + GROW) & 7
+        done[...] = done[...] * jnp.concatenate(
+            [
+                jnp.broadcast_to(scale[:, k * NP : (k + 1) * NP] * norm, (16, NP))
+                for k in range(N1)
+            ],
+            0,
+        )
+
+        @pl.when(band == h)
+        def _():
+            for k in range(N1):
+                for ch in range(WIDTH):
+                    lines[ch * HALF : (ch + 1) * HALF, :] = done[
+                        k * 16 : k * 16 + HALF, ch * LANES : (ch + 1) * LANES
+                    ]
+                col_out[k] = lines[...].astype(BF16)
+
+        def message(step):
+            target = jnp.where(band == 0, z + step, z - step + GROW) & 7
             for s in range(2):
                 block = done[pl.ds(pl.multiple_of((2 * target + s) * 16, 16), 16), :]
                 for ch in range(WIDTH):
                     at = (s * WIDTH + ch) * HALF
                     row_lines[at : at + HALF, :] = block[:HALF, ch * LANES : (ch + 1) * LANES]
-            row_outs[i][h] = row_lines[...].astype(BF16)
+            return row_lines[...].astype(BF16)
+
+        for step in range(1, 4):
+            row_outs[step][jnp.where(band == h, 0, 1)] = message(step)
+
+        @pl.when(band == h)
+        def _():
+            row_outs[4][0] = message(4)
+
+        @pl.when(band != h)
+        def _():
+            row_outs[0][0] = message(0)
 
 
 def stay(array):
@@ -228,11 +249,11 @@
     return pl.pallas_call(
         density_kernel,
         out_shape=[
-            jax.ShapeDtypeStruct((N1, 2, BLOCK, LANES), BF16),
+            jax.ShapeDtypeStruct((N1, BLOCK, LANES), BF16),
         ]
-        + [jax.ShapeDtypeStruct((2, ROWBLOCK, LANES), BF16)] * 4,
+        + [jax.ShapeDtypeStruct((n, ROWBLOCK, LANES), BF16) for n in (1, 2, 2, 2, 1)],
         in_specs=[smem] * 5 + [vmem, hbm, anywhere] + [hbm] * 7,
-        out_specs=[vmem] * 5,
+        out_specs=[vmem] * 6,
         scratch_shapes=[
             VMEM((8 * LINES, LANES), F32),
             VMEM((2 * HALF * M1, KP), BF16),
@@ -261,10 +282,12 @@
 
 
 def pack_kernel(*refs):
-    blocks, out, spread = refs[:4], refs[4], refs[5]
+    blocks, out, spread = refs[:5], refs[5], refs[6]
     stride = ROWBLOCK + 4
-    for v in range(8):
-        spread[v * stride : v * stride + ROWBLOCK, :] = blocks[v // 2][v % 2].astype(F32)
+    for i in range(4):
+        for m, block in enumerate((blocks[i + 1][0], blocks[i][1 if i else 0])):
+            at = (2 * i + m) * stride
+            spread[at : at + ROWBLOCK, :] = block.astype(F32)
     for ch in range(2 * WIDTH):
         for pp in range(HALF // 2):
             got = [spread[pl.ds(ch * HALF + 2 * pp + q, 8, stride=stride), :] for q in range(2)]
@@ -278,7 +301,7 @@
     return pl.pallas_call(
         pack_kernel,
         out_shape=jax.ShapeDtypeStruct((8 * HALF, ROW), BF16),
-        in_specs=[vmem] * 4,
+        in_specs=[vmem] * 5,
         out_specs=vmem,
         scratch_shapes=[VMEM((8 * (ROWBLOCK + 4), LANES), F32)],
         compiler_params=pltpu.CompilerParams(vmem_limit_bytes=4 << 20),
@@ -303,28 +326,14 @@
 
 
 def assemble_kernel(place, *refs):
-    cols = refs[:10]
-    away_out, home_out, spread = refs[10:]
+    cols = refs[:8]
+    away_out, home_out, spread = refs[8:]
     me = place[0]
     band, y, x = me >> 7, (me >> 2) & 3, me & 3
-
-    def take(part, first):
-        for i in range(4):
-            col = cols[part * 5 + first + i]
-            for q in range(GCOL // 2):
-                for h in range(2):
-                    at = (2 * i + h) * COLROWS + (part * 8 + q) * BLOCK
-                    spread[at : at + BLOCK, :] = col[q, h].astype(F32)
-
-    @pl.when(band == 0)
-    def _():
-        take(0, 1)
-        take(1, 0)
-
-    @pl.when(band == 1)
-    def _():
-        take(0, 0)
-        take(1, 1)
+    for v, col in enumerate(cols):
+        for q in range(GCOL):
+            at = v * COLROWS + q * BLOCK
+            spread[at : at + BLOCK, :] = col[q].astype(F32)
 
     def assemble(j, carry):
         outer, inner = around(j >> 2), around(j & 3)
@@ -363,7 +372,7 @@
     return pl.pallas_call(
         assemble_kernel,
         out_shape=[jax.ShapeDtypeStruct((PANEL, NP), BF16)] * 2,
-        in_specs=[pl.BlockSpec(memory_space=SMEM)] + [vmem] * 10,
+        in_specs=[pl.BlockSpec(memory_space=SMEM)] + [vmem] * 8,
         out_specs=[vmem] * 2,
         scratch_shapes=[VMEM((GROW * COLROWS, LANES), F32)],
         compiler_params=pltpu.CompilerParams(vmem_limit_bytes=14 << 20),
@@ -444,20 +453,13 @@
     return lax.ppermute(array, PLANE, pairs)
 
 
-ALL = ("band", "grow", "gcol_0", "gcol_1")
-
-
-def along(array, steps):
+def along(array, step):
     pairs = []
     for band in range(2):
-        for plane in range(GCOL):
-            step = steps((band == 0) == (plane < 8), band)
-            if step is None:
-                continue
-            for z in range(GROW):
-                to = (z + step) % GROW if band == 0 else (z - step) % GROW
-                pairs.append(((band * GROW + z) * GCOL + plane, (band * GROW + to) * GCOL + plane))
-    return lax.ppermute(array, ALL, pairs)
+        for z in range(GROW):
+            to = (z + step) % GROW if band == 0 else (z - step) % GROW
+            pairs.append((band * GROW + z, band * GROW + to))
+    return lax.ppermute(array, ("band", "grow"), pairs)
 
 
 def swap(array):
@@ -485,18 +487,17 @@
 
 
 def exchange(place, col, rows):
-    rows = [along(rows[i], lambda f, b, i=i: i + 1 if f else i) for i in range(4)]
+    rows = [rows[0]] + [along(rows[i], i) for i in range(1, 5)]
     col = lax.all_to_all(col, ("gcol_0", "gcol_1"), 0, 0, tiled=True)
     row = pack_call(rows)
-    parts = [col[:8], col[8:]]
+    main, other = [col], [swap(col)]
+    for _ in range(1, 5):
+        main.append(along(main[-1], 1))
+    for _ in range(1, 4):
+        other.append(along(other[-1], 1))
     rings = []
-    for part in range(2):
-        ring = [parts[part]]
-        for i in range(1, 5):
-            ring.append(
-                along(ring[-1], lambda f, b, i=i, part=part: 1 if i < 4 or b == part else None)
-            )
-        rings += ring
+    for i in range(4):
+        rings += [main[i + 1], other[i]]
     far = turned(row, 0, 2)
     below, above = turned(row, 0, 1), turned(row, 0, -1)
     line = jnp.concatenate([row, below, above, far], 0)

time: 116 us -> 119 us (1.026)
  blocking collectives: 0 us -> 18.5 us
  waiting for transfers between devices: 23.9 us -> 15.7 us
  starting transfers between devices: 55.5 us -> 48.2 us
    all_to_all x0 -> x1, blocking collectives: none -> 18.5 us  [exchange(): col = lax.all_to_all(col, ('gcol_0', 'gcol_1'), 0, 0, tiled=True)]
    ppermute x12 -> x11, starting transfers between devices: 17.8 us -> 27 us  [along(): return lax.ppermute(array, ('band', 'grow'), pairs)]
    ppermute x4 -> x5, starting transfers between devices: 19.8 us -> 12.2 us  [swap(): return lax.ppermute(array, 'band', [(0, 1), (1, 0)])]
    ppermute x12 -> x11, waiting for transfers between devices: 17.4 us -> 10 us  [along(): return lax.ppermute(array, ('band', 'grow'), pairs)]
    all_to_all x1 -> x0, waiting for transfers between devices: 6.03 us -> none  [exchange(): col = lax.all_to_all(col, ('gcol_0', 'gcol_1'), 0, 0, tiled=True)]
    ppermute x7, waiting for transfers between devices: 0.43 us -> 5.58 us  [turned(): return lax.ppermute(array, PLANE, pairs)]
    all_to_all x1 -> x0, starting transfers between devices: 5.06 us -> none  [exchange(): col = lax.all_to_all(col, ('gcol_0', 'gcol_1'), 0, 0, tiled=True)]
    ppermute x7, starting transfers between devices: 12.8 us -> 8.92 us  [turned(): return lax.ppermute(array, PLANE, pairs)]
  transfers between devices with their start and end apart: 24 -> 23, of which waited for: 10 -> 10; matrix products, arithmetic and copies ran while one was open for 0% -> 0% of each run, Pallas kernels for 8% -> 8%
where the time goes in v3:
time: 119 us
  starting transfers between devices  48.2 us (41%)
  Pallas kernels  27.5 us (23%)
  blocking collectives  18.5 us (16%)
  waiting for transfers between devices  15.7 us (13%)
  local copies, waits for them, and re-layouts  5.49 us (5%)
  other arithmetic  2.71 us (2%)
    ppermute x11, starting transfers between devices, along(): return lax.ppermute(array, ('band', 'grow'), pairs)  27 us
    all_to_all x1, blocking collectives, exchange(): col = lax.all_to_all(col, ('gcol_0', 'gcol_1'), 0, 0, tiled=True)  18.5 us
    ppermute x5, starting transfers between devices, swap(): return lax.ppermute(array, 'band', [(0, 1), (1, 0)])  12.2 us
    pallas_call x1, Pallas kernels, density_call(): pl.pallas_call(density_kernel, out_shape=[jax.ShapeDtypeStruct((N1, BLOCK...  12 us
    ppermute x11, waiting for transfers between devices, along(): return lax.ppermute(array, ('band', 'grow'), pairs)  10 us
    ppermute x7, starting transfers between devices, turned(): return lax.ppermute(array, PLANE, pairs)  8.92 us
    pallas_call x1, Pallas kernels, away_call(): pl.pallas_call(away_kernel, out_shape=(jax.ShapeDtypeStruct((ROW, NP), BF...  5.95 us
    ppermute x7, waiting for transfers between devices, turned(): return lax.ppermute(array, PLANE, pairs)  5.58 us
  transfers between devices with their start and end apart: 23, of which 10 were waited for; matrix products, arithmetic and copies ran while one was open for 0% of the time, Pallas kernels for 8%

profile of v3, /device:TPU:1, one launch (start us, length us, event | category | flops | bytes accessed | tf_op | source)
XLA Modules:
  0.0 118.8 jit_solution(17608170050880200550)
XLA Ops:
  0.0 3.2 %collective-permute-start.2 = (bf16[4,98304]{1,0:T(4,128)(2,1)}, bf16[4,98304]{1,0:T(4,128)(2,1)S(1)}, u32[]{:S(2)}, u32[]{:S(2)}) collective-permute-start(bf16[4,98304]{1,0:T(4,128)(2,1)} %refs_0_.1), channel_id=1, source_target_pairs={{0,128},{128,0},{1,129},{129,1},{2,130},{130,2},{3,131},{131,3},{4... | collective-permute-start | bytes 2359304 | tf_op jit(solution)/shard_map/ppermute | solution.py:466
  3.2 0.0 collective-permute-start.1
  3.2 0.5 collective-permute-start
  4.4 0.0 copy-start.2
  4.4 2.1 %ready.1.vals = f32[12352,128]{1,0:T(8,128)S(1)} custom-call(bf16[16,98304]{1,0:T(8,128)(2,1)} %source.1), custom_call_target="tpu_custom_call" | custom-call | tf_op jit(solution)/shard_map/ready/pallas_call | solution.py:83
  6.5 0.0 copy-start
  6.5 2.6 %copy-done = f32[12352,128]{1,0:T(8,128)} copy-done((f32[12352,128]{1,0:T(8,128)}, f32[12352,128]{1,0:T(8,128)S(1)}, u32[]{:S(2)}) %copy-start) | copy-done | bytes 6324248
  9.2 0.0 collective-permute-done.1.other_count
  9.2 0.0 collective-permute-done.other
  9.2 0.0 collective-permute-done.2.refs_1_
  9.2 0.0 copy-done.2
  9.2 0.0 copy-start.1
  9.2 2.8 %copy-done.1 = f32[12352,128]{1,0:T(8,128)S(1)} copy-done((f32[12352,128]{1,0:T(8,128)S(1)}, f32[12352,128]{1,0:T(8,128)}, u32[]{:S(2)}) %copy-start.1) | copy-done | bytes 6324248
  12.0 12.0 %density.1 = (bf16[16,64,128]{2,1,0:T(8,128)(2,1)S(1)}, bf16[1,120,128]{2,1,0:T(8,128)(2,1)S(1)}, bf16[2,120,128]{2,1,0:T(8,128)(2,1)S(1)}, bf16[2,120,128]{2,1,...) custom-call(s32[1]{0:T(128)} %bitcast.place, s32[2,20]{1,0:T(2,128)S(1)} %copy-done.2, ...), custom_call_target="tpu_custom_call" | custom-call | tf_op jit(solution)/shard_map/density/pallas_call | solution.py:249
  24.0 3.9 %collective-permute-start.11 = (bf16[2,120,128]{2,1,0:T(8,128)(2,1)S(1)}, bf16[2,120,128]{2,1,0:T(8,128)(2,1)S(1)}, u32[]{:S(2)}, u32[]{:S(2)}) collective-permute-start(bf16[2,120,128]{2,1,0:T(8,128)(2,1)S(1)} %get-tuple-element.19), channel_id=1, source_target_pairs={{0,16},{16,32},{32,48},{48,64},{64,80},{80,96},{96,112},{112,0},{1... | collective-permute-start | bytes 184328 | tf_op jit(solution)/shard_map/ppermute | solution.py:462
  28.0 1.1 collective-permute-start.12
  29.1 0.5 collective-permute-start.13
  29.6 4.4 %collective-permute-start.14 = (bf16[1,120,128]{2,1,0:T(8,128)(2,1)S(1)}, bf16[1,120,128]{2,1,0:T(8,128)(2,1)S(1)}, u32[]{:S(2)}, u32[]{:S(2)}) collective-permute-start(bf16[1,120,128]{2,1,0:T(8,128)(2,1)S(1)} %get-tuple-element.22), channel_id=1, source_target_pairs={{0,64},{16,80},{32,96},{48,112},{64,0},{80,16},{96,32},{112,48},{1... | collective-permute-start | bytes 92168 | tf_op jit(solution)/shard_map/ppermute | solution.py:462
  34.0 3.5 %collective-permute-done.14.refs_4_ = bf16[1,120,128]{2,1,0:T(8,128)(2,1)S(1)} collective-permute-done((bf16[1,120,128]{2,1,0:T(8,128)(2,1)S(1)}, bf16[1,120,128]{2,1,0:T(8,128)(2,1)S(1)}, u32[]{:S(2)}, u32[]{:S(2)}) %collective-permute-start.14) | collective-permute-done | bytes 30752 | tf_op jit(solution)/shard_map/ppermute | solution.py:462
  37.6 0.0 collective-permute-done.11.refs_1_
  37.6 0.0 collective-permute-done.12.refs_2_
  37.6 0.0 collective-permute-done.13.refs_3_
  37.6 0.1 pack.1
  37.7 3.0 %collective-permute-start.17 = (bf16[80,1536]{1,0:T(8,128)(2,1)S(1)}, bf16[80,1536]{1,0:T(8,128)(2,1)S(1)}, u32[]{:S(2)}, u32[]{:S(2)}) collective-permute-start(bf16[80,1536]{1,0:T(8,128)(2,1)S(1)} %pack.1), channel_id=1, source_target_pairs={{0,2},{1,3},{2,0},{3,1},{4,6},{5,7},{6,4},{7,5},{8,10},{9,11},{10,... | collective-permute-start | bytes 737288 | tf_op jit(solution)/shard_map/ppermute | solution.py:453
  40.7 0.8 collective-permute-start.16
  41.5 0.7 collective-permute-start.15
  42.1 2.4 %collective-permute-done.17 = bf16[80,1536]{1,0:T(8,128)(2,1)S(1)} collective-permute-done((bf16[80,1536]{1,0:T(8,128)(2,1)S(1)}, bf16[80,1536]{1,0:T(8,128)(2,1)S(1)}, u32[]{:S(2)}, u32[]{:S(2)}) %collective-permute-start.17) | collective-permute-done | bytes 245792 | tf_op jit(solution)/shard_map/ppermute | solution.py:453
  44.6 3.1 %collective-permute-done.16 = bf16[80,1536]{1,0:T(8,128)(2,1)S(1)} collective-permute-done((bf16[80,1536]{1,0:T(8,128)(2,1)S(1)}, bf16[80,1536]{1,0:T(8,128)(2,1)S(1)}, u32[]{:S(2)}, u32[]{:S(2)}) %collective-permute-start.16) | collective-permute-done | bytes 245792 | tf_op jit(solution)/shard_map/ppermute | solution.py:453
  47.7 0.1 collective-permute-done.15
  47.7 0.1 pad_maximum_fusion.refs_0_
  47.8 2.8 %collective-permute-start.19 = (bf16[320,1536]{1,0:T(8,128)(2,1)S(1)}, bf16[320,1536]{1,0:T(8,128)(2,1)S(1)}, u32[]{:S(2)}, u32[]{:S(2)}) collective-permute-start(bf16[320,1536]{1,0:T(8,128)(2,1)S(1)} %pad_maximum_fusion.refs_0_), channel_id=1, source_target_pairs={{0,12},{1,13},{2,14},{3,15},{4,0},{5,1},{6,2},{7,3},{8,4},{9,5},{1... | collective-permute-start | bytes 2949128 | tf_op jit(solution)/shard_map/ppermute | solution.py:453
  50.6 0.0 collective-permute-start.18
  50.6 18.5 %all_to_all.5 = bf16[16,64,128]{2,1,0:T(8,128)(2,1)S(1)} all-to-all(bf16[16,64,128]{2,1,0:T(8,128)(2,1)S(1)} %get-tuple-element.15), channel_id=1, replica_groups=mesh['band'=2,'grow'=8,'gcol_0'=4,'gcol_1'=4] {'gcol_0','gcol_1'}, dimensions={0} | all-to-all | bytes 524288 | tf_op jit(solution)/shard_map/all_to_all | solution.py:491
  69.1 3.4 %collective-permute-start.4 = (bf16[16,64,128]{2,1,0:T(8,128)(2,1)S(1)}, bf16[16,64,128]{2,1,0:T(8,128)(2,1)S(1)}, u32[]{:S(2)}, u32[]{:S(2)}) collective-permute-start(bf16[16,64,128]{2,1,0:T(8,128)(2,1)S(1)} %all_to_all.5), channel_id=1, source_target_pairs={{0,128},{128,0},{1,129},{129,1},{2,130},{130,2},{3,131},{131,3},{4... | collective-permute-start | bytes 786440 | tf_op jit(solution)/shard_map/ppermute | solution.py:466
  72.4 2.6 %collective-permute-start.3 = (bf16[16,64,128]{2,1,0:T(8,128)(2,1)S(1)}, bf16[16,64,128]{2,1,0:T(8,128)(2,1)S(1)}, u32[]{:S(2)}, u32[]{:S(2)}) collective-permute-start(bf16[16,64,128]{2,1,0:T(8,128)(2,1)S(1)} %all_to_all.5), channel_id=1, source_target_pairs={{0,16},{16,32},{32,48},{48,64},{64,80},{80,96},{96,112},{112,0},{1... | collective-permute-start | bytes 786440 | tf_op jit(solution)/shard_map/ppermute | solution.py:462
  75.1 0.0 collective-permute-done.4.refs_1_
  75.1 1.2 collective-permute-start.6
  76.2 2.2 %collective-permute-done.3.refs_0_ = bf16[16,64,128]{2,1,0:T(8,128)(2,1)S(1)} collective-permute-done((bf16[16,64,128]{2,1,0:T(8,128)(2,1)S(1)}, bf16[16,64,128]{2,1,0:T(8,128)(2,1)S(1)}, u32[]{:S(2)}, u32[]{:S(2)}) %collective-permute-start.3) | collective-permute-done | bytes 262176 | tf_op jit(solution)/shard_map/ppermute | solution.py:462
  78.4 3.1 %collective-permute-start.5 = (bf16[16,64,128]{2,1,0:T(8,128)(2,1)S(1)}, bf16[16,64,128]{2,1,0:T(8,128)(2,1)S(1)}, u32[]{:S(2)}, u32[]{:S(2)}) collective-permute-start(bf16[16,64,128]{2,1,0:T(8,128)(2,1)S(1)} %collective-permute-done.3.refs_0_), channel_id=1, source_target_pairs={{0,16},{16,32},{32,48},{48,64},{64,80},{80,96},{96,112},{112,0},{1... | collective-permute-start | bytes 786440 | tf_op jit(solution)/shard_map/ppermute | solution.py:462
  81.5 0.0 collective-permute-done.6.refs_3_
  81.5 2.8 %collective-permute-start.8 = (bf16[16,64,128]{2,1,0:T(8,128)(2,1)S(1)}, bf16[16,64,128]{2,1,0:T(8,128)(2,1)S(1)}, u32[]{:S(2)}, u32[]{:S(2)}) collective-permute-start(bf16[16,64,128]{2,1,0:T(8,128)(2,1)S(1)} %collective-permute-done.6.refs_3_), channel_id=1, source_target_pairs={{0,16},{16,32},{32,48},{48,64},{64,80},{80,96},{96,112},{112,0},{1... | collective-permute-start | bytes 786440 | tf_op jit(solution)/shard_map/ppermute | solution.py:462
  84.3 0.5 collective-permute-done.5.refs_2_
  84.8 3.1 %collective-permute-start.7 = (bf16[16,64,128]{2,1,0:T(8,128)(2,1)S(1)}, bf16[16,64,128]{2,1,0:T(8,128)(2,1)S(1)}, u32[]{:S(2)}, u32[]{:S(2)}) collective-permute-start(bf16[16,64,128]{2,1,0:T(8,128)(2,1)S(1)} %collective-permute-done.5.refs_2_), channel_id=1, source_target_pairs={{0,16},{16,32},{32,48},{48,64},{64,80},{80,96},{96,112},{112,0},{1... | collective-permute-start | bytes 786440 | tf_op jit(solution)/shard_map/ppermute | solution.py:462
  87.9 0.0 collective-permute-done.19.refs_2_
  88.0 1.3 %collective-permute-start.21 = (bf16[160,1536]{1,0:T(8,128)(2,1)S(1)}, bf16[160,1536]{1,0:T(8,128)(2,1)S(1)}, u32[]{:S(2)}, u32[]{:S(2)}) collective-permute-start(bf16[160,1536]{1,0:T(8,128)(2,1)S(1)} %slice.9), channel_id=1, source_target_pairs={{0,12},{1,13},{2,14},{3,15},{4,0},{5,1},{6,2},{7,3},{8,4},{9,5},{1... | collective-permute-start | bytes 1474568 | tf_op jit(solution)/shard_map/ppermute | solution.py:453
  89.3 0.0 collective-permute-done.18.refs_1_
  89.3 0.3 collective-permute-start.20
  89.7 0.0 collective-permute-done.8.refs_5_
  89.7 1.1 collective-permute-start.10
  90.8 0.5 collective-permute-done.7.refs_4_
  91.3 3.1 %collective-permute-start.9 = (bf16[16,64,128]{2,1,0:T(8,128)(2,1)S(1)}, bf16[16,64,128]{2,1,0:T(8,128)(2,1)S(1)}, u32[]{:S(2)}, u32[]{:S(2)}) collective-permute-start(bf16[16,64,128]{2,1,0:T(8,128)(2,1)S(1)} %collective-permute-done.7.refs_4_), channel_id=1, source_target_pairs={{0,16},{16,32},{32,48},{48,64},{64,80},{80,96},{96,112},{112,0},{1... | collective-permute-start | bytes 786440 | tf_op jit(solution)/shard_map/ppermute | solution.py:462
  94.4 0.8 collective-permute-done.10.refs_7_
  95.2 2.5 %collective-permute-done.9.refs_6_ = bf16[16,64,128]{2,1,0:T(8,128)(2,1)S(1)} collective-permute-done((bf16[16,64,128]{2,1,0:T(8,128)(2,1)S(1)}, bf16[16,64,128]{2,1,0:T(8,128)(2,1)S(1)}, u32[]{:S(2)}, u32[]{:S(2)}) %collective-permute-start.9) | collective-permute-done | bytes 262176 | tf_op jit(solution)/shard_map/ppermute | solution.py:462
  97.7 3.2 %assemble.1 = (bf16[1280,768]{1,0:T(8,128)(2,1)S(1)}, bf16[1280,768]{1,0:T(8,128)(2,1)S(1)}) custom-call(s32[1]{0:T(128)} %bitcast.place, bf16[16,64,128]{2,1,0:T(8,128)(2,1)S(1)} %collective-permute-done.3.refs_0_, bf16[16,64,128]{2,1,0:T(8,128)(2,1)S(1)} %collective-permute-done.4.refs_1_, bf16[16,64,128]{2,1,0:T(8,128)(2,1)S(1)} %collective-permute-done.5.refs_2_, ...), custom_call_target="tpu_custom_call" | custom-call | tf_op jit(solution)/shard_map/assemble/pallas_call | solution.py:372
  100.9 0.0 collective-permute-done.21.refs_4_
  100.9 0.0 collective-permute-done.20.refs_3_
  100.9 5.9 %away.1 = (bf16[1536,768]{1,0:T(8,128)(2,1)S(1)}, bf16[1536,1280]{1,0:T(8,128)(2,1)S(1)}) custom-call(bf16[1280,768]{1,0:T(8,128)(2,1)S(1)} %get-tuple-element.17.weighted, bf16[320,1536]{1,0:T(8,128)(2,1)S(1)} %pad_maximum_fusion.refs_0_, bf16[320,1536]{1,0:T(8,128)(2,1)S(1)} %collective-permute-done.18.refs_1_, ...), custom_call_target="tpu_custom_call" | custom-call | tf_op jit(solution)/shard_map/away/pallas_call | solution.py:405
  106.9 5.2 %collective-permute-start.22 = (bf16[1536,768]{1,0:T(8,128)(2,1)S(1)}, bf16[1536,768]{1,0:T(8,128)(2,1)S(1)}, u32[]{:S(2)}, u32[]{:S(2)}) collective-permute-start(bf16[1536,768]{1,0:T(8,128)(2,1)S(1)} %get-tuple-element.24), channel_id=1, source_target_pairs={{0,128},{128,0},{1,129},{129,1},{2,130},{130,2},{3,131},{131,3},{4... | collective-permute-start | bytes 7077896 | tf_op jit(solution)/shard_map/ppermute | solution.py:466
  112.0 4.1 %home.1 = f32[1536,768]{1,0:T(8,128)S(1)} custom-call(bf16[1280,768]{1,0:T(8,128)(2,1)S(1)} %get-tuple-element.16.weighted, bf16[1536,1280]{1,0:T(8,128)(2,1)S(1)} %get-tuple-element.23.rows), custom_call_target="tpu_custom_call" | custom-call | tf_op jit(solution)/shard_map/home/pallas_call | solution.py:431
  116.1 0.1 collective-permute-done.22
  116.2 2.6 %negate_bitcast_fusion = f32[1,1536,768]{2,1,0:T(8,128)} fusion(f32[1536,768]{1,0:T(8,128)S(1)} %home.1, bf16[1536,768]{1,0:T(8,128)(2,1)S(1)} %collective-permute-done.22), kind=kLoop, calls=%fused_computation | loop fusion | flops 3538944 | bytes 11796480 | tf_op jit(solution)/shard_map/neg | solution.py:512
  (2 shorter events, 0.1 us)
Async XLA Ops:
  0.0 9.2 %collective-permute-start.2 = (bf16[4,98304]{1,0:T(4,128)(2,1)}, bf16[4,98304]{1,0:T(4,128)(2,1)S(1)}, u32[]{:S(2)}, u32[]{:S(2)}) collective-permute-start(bf16[4,98304]{1,0:T(4,128)(2,1)} %refs_0_.1), channel_id=1, source_target_pairs={{0,128},{128,0},{1,129},{129,1},{2,130},{130,2},{3,131},{131,3},{4... | collective-permute-start | bytes 2359304 | tf_op jit(solution)/shard_map/ppermute | solution.py:466
  3.2 6.0 %collective-permute-start.1 = (s32[1]{0:T(128)}, s32[1]{0:T(128)}, u32[]{:S(2)}, u32[]{:S(2)}) collective-permute-start(s32[1]{0:T(128)} %param.17), channel_id=1, source_target_pairs={{0,128},{128,0},{1,129},{129,1},{2,130},{130,2},{3,131},{131,3},{4... | collective-permute-start | bytes 20 | tf_op jit(solution)/shard_map/ppermute | solution.py:466
  3.2 6.0 %collective-permute-start = (s32[2,20]{1,0:T(2,128)}, s32[2,20]{1,0:T(2,128)S(1)}, u32[]{:S(2)}, u32[]{:S(2)}) collective-permute-start(s32[2,20]{1,0:T(2,128)} %mine.1), channel_id=1, source_target_pairs={{0,128},{128,0},{1,129},{129,1},{2,130},{130,2},{3,131},{131,3},{4... | collective-permute-start | bytes 488 | tf_op jit(solution)/shard_map/ppermute | solution.py:466
  4.4 4.8 %copy-start.2 = (s32[2,20]{1,0:T(2,128)S(1)}, s32[2,20]{1,0:T(2,128)}, u32[]{:S(2)}) copy-start(s32[2,20]{1,0:T(2,128)} %mine.1) | copy-start | bytes 484
  6.5 2.6 %copy-start = (f32[12352,128]{1,0:T(8,128)}, f32[12352,128]{1,0:T(8,128)S(1)}, u32[]{:S(2)}) copy-start(f32[12352,128]{1,0:T(8,128)S(1)} %ready.1.vals) | copy-start | bytes 18972676
  9.2 2.8 %copy-start.1 = (f32[12352,128]{1,0:T(8,128)S(1)}, f32[12352,128]{1,0:T(8,128)}, u32[]{:S(2)}) copy-start(f32[12352,128]{1,0:T(8,128)} %copy-done) | copy-start | bytes 18972676
  24.0 13.5 %collective-permute-start.11 = (bf16[2,120,128]{2,1,0:T(8,128)(2,1)S(1)}, bf16[2,120,128]{2,1,0:T(8,128)(2,1)S(1)}, u32[]{:S(2)}, u32[]{:S(2)}) collective-permute-start(bf16[2,120,128]{2,1,0:T(8,128)(2,1)S(1)} %get-tuple-element.19), channel_id=1, source_target_pairs={{0,16},{16,32},{32,48},{48,64},{64,80},{80,96},{96,112},{112,0},{1... | collective-permute-start | bytes 184328 | tf_op jit(solution)/shard_map/ppermute | solution.py:462
  28.0 9.6 %collective-permute-start.12 = (bf16[2,120,128]{2,1,0:T(8,128)(2,1)S(1)}, bf16[2,120,128]{2,1,0:T(8,128)(2,1)S(1)}, u32[]{:S(2)}, u32[]{:S(2)}) collective-permute-start(bf16[2,120,128]{2,1,0:T(8,128)(2,1)S(1)} %get-tuple-element.20), channel_id=1, source_target_pairs={{0,32},{16,48},{32,64},{48,80},{64,96},{80,112},{96,0},{112,16},{1... | collective-permute-start | bytes 184328 | tf_op jit(solution)/shard_map/ppermute | solution.py:462
  29.1 8.5 %collective-permute-start.13 = (bf16[2,120,128]{2,1,0:T(8,128)(2,1)S(1)}, bf16[2,120,128]{2,1,0:T(8,128)(2,1)S(1)}, u32[]{:S(2)}, u32[]{:S(2)}) collective-permute-start(bf16[2,120,128]{2,1,0:T(8,128)(2,1)S(1)} %get-tuple-element.21), channel_id=1, source_target_pairs={{0,48},{16,64},{32,80},{48,96},{64,112},{80,0},{96,16},{112,32},{1... | collective-permute-start | bytes 184328 | tf_op jit(solution)/shard_map/ppermute | solution.py:462
  29.6 8.0 %collective-permute-start.14 = (bf16[1,120,128]{2,1,0:T(8,128)(2,1)S(1)}, bf16[1,120,128]{2,1,0:T(8,128)(2,1)S(1)}, u32[]{:S(2)}, u32[]{:S(2)}) collective-permute-start(bf16[1,120,128]{2,1,0:T(8,128)(2,1)S(1)} %get-tuple-element.22), channel_id=1, source_target_pairs={{0,64},{16,80},{32,96},{48,112},{64,0},{80,16},{96,32},{112,48},{1... | collective-permute-start | bytes 92168 | tf_op jit(solution)/shard_map/ppermute | solution.py:462
  37.7 6.9 %collective-permute-start.17 = (bf16[80,1536]{1,0:T(8,128)(2,1)S(1)}, bf16[80,1536]{1,0:T(8,128)(2,1)S(1)}, u32[]{:S(2)}, u32[]{:S(2)}) collective-permute-start(bf16[80,1536]{1,0:T(8,128)(2,1)S(1)} %pack.1), channel_id=1, source_target_pairs={{0,2},{1,3},{2,0},{3,1},{4,6},{5,7},{6,4},{7,5},{8,10},{9,11},{10,... | collective-permute-start | bytes 737288 | tf_op jit(solution)/shard_map/ppermute | solution.py:453
  40.7 7.0 %collective-permute-start.16 = (bf16[80,1536]{1,0:T(8,128)(2,1)S(1)}, bf16[80,1536]{1,0:T(8,128)(2,1)S(1)}, u32[]{:S(2)}, u32[]{:S(2)}) collective-permute-start(bf16[80,1536]{1,0:T(8,128)(2,1)S(1)} %pack.1), channel_id=1, source_target_pairs={{0,3},{1,0},{2,1},{3,2},{4,7},{5,4},{6,5},{7,6},{8,11},{9,8},{10,9... | collective-permute-start | bytes 737288 | tf_op jit(solution)/shard_map/ppermute | solution.py:453
  41.5 6.3 %collective-permute-start.15 = (bf16[80,1536]{1,0:T(8,128)(2,1)S(1)}, bf16[80,1536]{1,0:T(8,128)(2,1)S(1)}, u32[]{:S(2)}, u32[]{:S(2)}) collective-permute-start(bf16[80,1536]{1,0:T(8,128)(2,1)S(1)} %pack.1), channel_id=1, source_target_pairs={{0,1},{1,2},{2,3},{3,0},{4,5},{5,6},{6,7},{7,4},{8,9},{9,10},{10,1... | collective-permute-start | bytes 737288 | tf_op jit(solution)/shard_map/ppermute | solution.py:453
  47.8 40.2 %collective-permute-start.19 = (bf16[320,1536]{1,0:T(8,128)(2,1)S(1)}, bf16[320,1536]{1,0:T(8,128)(2,1)S(1)}, u32[]{:S(2)}, u32[]{:S(2)}) collective-permute-start(bf16[320,1536]{1,0:T(8,128)(2,1)S(1)} %pad_maximum_fusion.refs_0_), channel_id=1, source_target_pairs={{0,12},{1,13},{2,14},{3,15},{4,0},{5,1},{6,2},{7,3},{8,4},{9,5},{1... | collective-permute-start | bytes 2949128 | tf_op jit(solution)/shard_map/ppermute | solution.py:453
  50.6 38.7 %collective-permute-start.18 = (bf16[320,1536]{1,0:T(8,128)(2,1)S(1)}, bf16[320,1536]{1,0:T(8,128)(2,1)S(1)}, u32[]{:S(2)}, u32[]{:S(2)}) collective-permute-start(bf16[320,1536]{1,0:T(8,128)(2,1)S(1)} %pad_maximum_fusion.refs_0_), channel_id=1, source_target_pairs={{0,4},{1,5},{2,6},{3,7},{4,8},{5,9},{6,10},{7,11},{8,12},{9,13},{1... | collective-permute-start | bytes 2949128 | tf_op jit(solution)/shard_map/ppermute | solution.py:453
  69.1 6.0 %collective-permute-start.4 = (bf16[16,64,128]{2,1,0:T(8,128)(2,1)S(1)}, bf16[16,64,128]{2,1,0:T(8,128)(2,1)S(1)}, u32[]{:S(2)}, u32[]{:S(2)}) collective-permute-start(bf16[16,64,128]{2,1,0:T(8,128)(2,1)S(1)} %all_to_all.5), channel_id=1, source_target_pairs={{0,128},{128,0},{1,129},{129,1},{2,130},{130,2},{3,131},{131,3},{4... | collective-permute-start | bytes 786440 | tf_op jit(solution)/shard_map/ppermute | solution.py:466
  72.4 6.0 %collective-permute-start.3 = (bf16[16,64,128]{2,1,0:T(8,128)(2,1)S(1)}, bf16[16,64,128]{2,1,0:T(8,128)(2,1)S(1)}, u32[]{:S(2)}, u32[]{:S(2)}) collective-permute-start(bf16[16,64,128]{2,1,0:T(8,128)(2,1)S(1)} %all_to_all.5), channel_id=1, source_target_pairs={{0,16},{16,32},{32,48},{48,64},{64,80},{80,96},{96,112},{112,0},{1... | collective-permute-start | bytes 786440 | tf_op jit(solution)/shard_map/ppermute | solution.py:462
  75.1 6.4 %collective-permute-start.6 = (bf16[16,64,128]{2,1,0:T(8,128)(2,1)S(1)}, bf16[16,64,128]{2,1,0:T(8,128)(2,1)S(1)}, u32[]{:S(2)}, u32[]{:S(2)}) collective-permute-start(bf16[16,64,128]{2,1,0:T(8,128)(2,1)S(1)} %collective-permute-done.4.refs_1_), channel_id=1, source_target_pairs={{0,16},{16,32},{32,48},{48,64},{64,80},{80,96},{96,112},{112,0},{1... | collective-permute-start | bytes 786440 | tf_op jit(solution)/shard_map/ppermute | solution.py:462
  78.4 6.4 %collective-permute-start.5 = (bf16[16,64,128]{2,1,0:T(8,128)(2,1)S(1)}, bf16[16,64,128]{2,1,0:T(8,128)(2,1)S(1)}, u32[]{:S(2)}, u32[]{:S(2)}) collective-permute-start(bf16[16,64,128]{2,1,0:T(8,128)(2,1)S(1)} %collective-permute-done.3.refs_0_), channel_id=1, source_target_pairs={{0,16},{16,32},{32,48},{48,64},{64,80},{80,96},{96,112},{112,0},{1... | collective-permute-start | bytes 786440 | tf_op jit(solution)/shard_map/ppermute | solution.py:462
  81.5 8.1 %collective-permute-start.8 = (bf16[16,64,128]{2,1,0:T(8,128)(2,1)S(1)}, bf16[16,64,128]{2,1,0:T(8,128)(2,1)S(1)}, u32[]{:S(2)}, u32[]{:S(2)}) collective-permute-start(bf16[16,64,128]{2,1,0:T(8,128)(2,1)S(1)} %collective-permute-done.6.refs_3_), channel_id=1, source_target_pairs={{0,16},{16,32},{32,48},{48,64},{64,80},{80,96},{96,112},{112,0},{1... | collective-permute-start | bytes 786440 | tf_op jit(solution)/shard_map/ppermute | solution.py:462
  84.8 6.4 %collective-permute-start.7 = (bf16[16,64,128]{2,1,0:T(8,128)(2,1)S(1)}, bf16[16,64,128]{2,1,0:T(8,128)(2,1)S(1)}, u32[]{:S(2)}, u32[]{:S(2)}) collective-permute-start(bf16[16,64,128]{2,1,0:T(8,128)(2,1)S(1)} %collective-permute-done.5.refs_2_), channel_id=1, source_target_pairs={{0,16},{16,32},{32,48},{48,64},{64,80},{80,96},{96,112},{112,0},{1... | collective-permute-start | bytes 786440 | tf_op jit(solution)/shard_map/ppermute | solution.py:462
  88.0 12.9 %collective-permute-start.21 = (bf16[160,1536]{1,0:T(8,128)(2,1)S(1)}, bf16[160,1536]{1,0:T(8,128)(2,1)S(1)}, u32[]{:S(2)}, u32[]{:S(2)}) collective-permute-start(bf16[160,1536]{1,0:T(8,128)(2,1)S(1)} %slice.9), channel_id=1, source_target_pairs={{0,12},{1,13},{2,14},{3,15},{4,0},{5,1},{6,2},{7,3},{8,4},{9,5},{1... | collective-permute-start | bytes 1474568 | tf_op jit(solution)/shard_map/ppermute | solution.py:453
  89.3 11.6 %collective-permute-start.20 = (bf16[160,1536]{1,0:T(8,128)(2,1)S(1)}, bf16[160,1536]{1,0:T(8,128)(2,1)S(1)}, u32[]{:S(2)}, u32[]{:S(2)}) collective-permute-start(bf16[160,1536]{1,0:T(8,128)(2,1)S(1)} %slice.8), channel_id=1, source_target_pairs={{0,4},{1,5},{2,6},{3,7},{4,8},{5,9},{6,10},{7,11},{8,12},{9,13},{1... | collective-permute-start | bytes 1474568 | tf_op jit(solution)/shard_map/ppermute | solution.py:453
  89.7 5.5 %collective-permute-start.10 = (bf16[16,64,128]{2,1,0:T(8,128)(2,1)S(1)}, bf16[16,64,128]{2,1,0:T(8,128)(2,1)S(1)}, u32[]{:S(2)}, u32[]{:S(2)}) collective-permute-start(bf16[16,64,128]{2,1,0:T(8,128)(2,1)S(1)} %collective-permute-done.8.refs_5_), channel_id=1, source_target_pairs={{0,16},{16,32},{32,48},{48,64},{64,80},{80,96},{96,112},{112,0},{1... | collective-permute-start | bytes 786440 | tf_op jit(solution)/shard_map/ppermute | solution.py:462
  91.3 6.4 %collective-permute-start.9 = (bf16[16,64,128]{2,1,0:T(8,128)(2,1)S(1)}, bf16[16,64,128]{2,1,0:T(8,128)(2,1)S(1)}, u32[]{:S(2)}, u32[]{:S(2)}) collective-permute-start(bf16[16,64,128]{2,1,0:T(8,128)(2,1)S(1)} %collective-permute-done.7.refs_4_), channel_id=1, source_target_pairs={{0,16},{16,32},{32,48},{48,64},{64,80},{80,96},{96,112},{112,0},{1... | collective-permute-start | bytes 786440 | tf_op jit(solution)/shard_map/ppermute | solution.py:462
  106.9 9.3 %collective-permute-start.22 = (bf16[1536,768]{1,0:T(8,128)(2,1)S(1)}, bf16[1536,768]{1,0:T(8,128)(2,1)S(1)}, u32[]{:S(2)}, u32[]{:S(2)}) collective-permute-start(bf16[1536,768]{1,0:T(8,128)(2,1)S(1)} %get-tuple-element.24), channel_id=1, source_target_pairs={{0,128},{128,0},{1,129},{129,1},{2,130},{130,2},{3,131},{131,3},{4... | collective-permute-start | bytes 7077896 | tf_op jit(solution)/shard_map/ppermute | solution.py:466
